TPU v7x, 32 devices: a whole 2x2x4 slice. The times are simulated.
32 devices in a mesh: blk: 8 (over z, y), lon: 4 (over x, core).
Axes of the slice: x: 2, y: 2, z: 4, core: 2. Of those that a mesh axis runs over, the one named last changes fastest.
Arguments:
- anomalies: float32 [16, 1152, 4320], P(None, 'blk', 'lon'), may hold values from -6 to 6
- classes: int32 [1152, 4320], P('blk', 'lon'), may hold values from 0 to 3
- legendre: float32 [32, 2160, 1152], P('blk', 'lon'), may hold values from -0.0234375 to 0.0234375
- precond: float32 [32, 16, 135, 135], P('blk', 'lon'), may hold values from -1 to 2, as said below
- prior: float32 [2160], P('lon'), may hold values from 0.05 to 0.5
- assign: int32 [32], replicated, may hold values from 0 to 31, as said below
Outputs:
- solution: float32 [32, 2, 16, 2160], P('blk', None, None, 'lon')
- residual: float32 [32, 2, 16, 2160], P('blk', None, None, 'lon')
Inputs may be any that keep to these rules, and one draw needn't show every extreme that they name: `assign`: A permutation of the order indices; the 4 slots of each index of blk hold 2 pairs q and 31 - q. `precond`: each block is symmetric, and its diagonal entries exceed the sum of the magnitudes of the other entries of their row.
All inputs are finite; a program needn't handle non-finite values.
Results may differ from a plain program's by a relative error of at most 0.00026.
Values sent between devices are 32-bit elements; how exact they have to be, the bound alone decides.
A program may use at most 128 MiB of HBM per device.

v0:
```python
import math

import jax
import jax.numpy as jnp
from jax import lax
from jax.sharding import PartitionSpec as P

ITERS = 2


HUBER_LEVELS = (1.0, 0.5, 0.25, 0.125)
HIGHEST = lax.Precision.HIGHEST


def build_mask(orders, first_degree, degrees):
    degree = first_degree + jnp.arange(degrees, dtype=jnp.int32)
    upper_part = (degree[None, :] >= orders[:, None]).astype(jnp.float32)
    sine_keep = upper_part * (orders[:, None] > 0).astype(jnp.float32)
    return jnp.stack([upper_part, sine_keep], axis=1)[:, :, None, :]


def trig_table(orders, first_col, columns, lon_total):
    column = first_col + jnp.arange(columns, dtype=jnp.int32)
    phases = orders[:, None] * column[None, :] % lon_total
    angles = phases.astype(jnp.float32) * (2.0 * math.pi / lon_total)
    return jnp.stack([jnp.cos(angles), jnp.sin(angles)], axis=1)


def huber_weights(classes):
    weighted = jnp.zeros(classes.shape, jnp.float32)
    for level_index in range(4):
        weighted = (
            weighted + (classes == level_index).astype(jnp.float32) * HUBER_LEVELS[level_index]
        )
    return weighted


def legendre_up(coeffs, basis_rows):
    return jnp.einsum("scnl,slr->scnr", coeffs, basis_rows, precision=HIGHEST)


def legendre_down(cycles_part, basis_rows):
    return jnp.einsum("scnr,slr->scnl", cycles_part, basis_rows, precision=HIGHEST)


def body(anomalies, classes, legendre, precond, prior, assign):
    lon_count = lax.axis_size("lon")
    blk_count = lax.axis_size("blk")
    blk_place = lax.axis_index("blk")
    lon_place = lax.axis_index("lon")
    slot_count = legendre.shape[0]
    local_degrees = legendre.shape[1]
    rhs_count = anomalies.shape[0]
    cycle_count = anomalies.shape[1]
    longitudes = anomalies.shape[2]
    window = assign.shape[0]
    block_width = precond.shape[2]
    quarter = slot_count // lon_count
    grid_rows = rhs_count * cycle_count
    stride_value = local_degrees * lon_count // window
    all_orders = assign * stride_value
    own_orders = lax.dynamic_slice_in_dim(all_orders, blk_place * slot_count, slot_count)
    first_degree = lon_place * local_degrees
    first_column = lon_place * longitudes
    live_mask = build_mask(own_orders, first_degree, local_degrees)
    weights = huber_weights(classes)
    row_orders = (
        all_orders.reshape(blk_count, lon_count, quarter).transpose(1, 0, 2).reshape(window)
    )
    trig_rows = trig_table(row_orders, first_column, longitudes, longitudes * lon_count).reshape(
        2 * window, longitudes
    )

    def analyse(grid_field):
        flat_grid = grid_field.reshape(grid_rows, longitudes)
        product = lax.dot_general(trig_rows, flat_grid, (((1,), (1,)), ((), ())), precision=HIGHEST)
        shared = lax.psum_scatter(
            product.reshape(window // lon_count * lax.axis_size("lon"), 2, rhs_count, cycle_count),
            "lon",
            scatter_dimension=0,
            tiled=True,
        )
        returned = lax.all_to_all(shared, "blk", split_axis=0, concat_axis=3, tiled=True)
        return legendre_down(lax.all_gather(returned, "lon", axis=0, tiled=True), legendre)

    def precondition(coeffs):
        blocks = coeffs.reshape(slot_count, 2, rhs_count, local_degrees // block_width, block_width)
        applied = jnp.einsum("sbij,scnbj->scnbi", precond, blocks, precision=HIGHEST)
        return live_mask * applied.reshape(coeffs.shape)

    def column_dot(lhs_values, rhs_values):
        return jnp.sum(lhs_values * rhs_values, axis=(0, 1, 3))

    def spread(values):
        return values[None, None, :, None]

    def fit_sum(lhs_values, rhs_values):
        return lax.psum(column_dot(lhs_values, rhs_values), ("blk", "lon"))

    residual = live_mask * analyse(weights * anomalies)
    solution = jnp.zeros_like(residual)
    search = precondition(residual)
    fit_now = fit_sum(residual, search)
    direction = search
    for iteration in range(ITERS):
        synthesize_coeffs = direction
        synthesize_shared = lax.psum_scatter(
            legendre_up(synthesize_coeffs, legendre), "lon", scatter_dimension=0, tiled=True
        )
        moved = lax.all_to_all(synthesize_shared, "blk", split_axis=3, concat_axis=0, tiled=True)
        flat_orders = lax.all_gather(moved, "lon", axis=0, tiled=True).reshape(-1, grid_rows)
        grid_flat = lax.dot_general(
            flat_orders, trig_rows, (((0,), (0,)), ((), ())), precision=HIGHEST
        )
        image_vec = live_mask * (
            analyse(weights * grid_flat.reshape(rhs_count, cycle_count, longitudes))
            + prior * direction
        )
        curvature_sum = lax.psum(column_dot(direction, image_vec), ("blk", "lon"))
        alpha_step = fit_now / curvature_sum
        solution = solution + spread(alpha_step) * direction
        residual = residual - spread(alpha_step) * image_vec
        if iteration + 1 < ITERS:
            search = precondition(residual)
            fit_next = fit_sum(residual, search)
            direction = search + spread(fit_next / fit_now) * direction
            fit_now = fit_next
    return (solution, residual)


def solution(mesh):
    in_specs = (
        P(None, "blk", "lon"),
        P("blk", "lon"),
        P("blk", "lon", None),
        P("blk", "lon", None, None),
        P("lon"),
        P(),
    )
    out_specs = (P("blk", None, None, "lon"), P("blk", None, None, "lon"))
    return jax.shard_map(body, mesh=mesh, in_specs=in_specs, out_specs=out_specs, check_vma=False)
```

profile of v0, /device:TPU:0, one launch (start us, length us, event | category | flops | bytes accessed | tf_op | source)
XLA Modules:
  0.0 575.7 jit_solution(8093383690541795025)
XLA Ops:
  10.3 15.7 %fusion.4 = f32[32,2,16,144]{3,0,2,1:T(8,128)} fusion(f32[16,144,1080]{2,1,0:T(8,128)} %param.6, f32[144,1080]{1,0:T(8,128)S(1)} %select_add_fusion, f32[32,1,1080]{2,0,1:T(8,128)S(1)} %get-tuple-element.9, f32[32,1,1080]{2,0,1:T(8,128)S(1)} %get-tuple-element.8), kind=kOutput, calls=%fused_computation.4 | convolution fusion | flops 1913587200 | bytes 11441664 | tf_op jit(solution)/shard_map/dot_general | solution.py:76
  26.2 27.5 %reduce-scatter.6.cloned.1.call-done = f32[8,2,16,144]{3,0,2,1:T(8,128)} async-done(((f32[32,2,16,144]{3,0,2,1:T(8,128)}), f32[8,2,16,144]{3,0,2,1:T(8,128)}) %reduce-scatter.6.cloned.1.call-update) | async-done | bytes 147472 | tf_op jit(solution)/shard_map/reduce_scatter | solution.py:77
  55.5 5.5 all-to-all-start
  61.1 8.6 %all-to-all-done = f32[8,2,16,144]{3,2,1,0:T(8,128)S(1)} async-done(((f32[8,2,16,144]{3,2,1,0:T(8,128)}), f32[8,2,16,144]{3,2,1,0:T(8,128)S(1)}, u32[]{:S(2)}, u32[]{:S(2)}) %all-to-all-start) | async-done | bytes 147488 | tf_op jit(solution)/shard_map/all_to_all | solution.py:83
  71.7 6.7 %all_gather.15 = f32[4,2,16,1152]{3,2,1,0:T(8,128)S(1)} all-gather(f32[1,2,16,1152]{3,2,1,0:T(8,128)S(1)} %all_to_all.68), channel_id=1, replica_groups=mesh['blk'=8,'lon'=4] {'lon'}, dimensions={0}, use_global_device_ids=true | all-gather | bytes 737280 | tf_op jit(solution)/shard_map/all_gather | solution.py:84
  78.4 17.2 %fusion.32 = f32[4,2,16,540]{3,2,1,0:T(8,128)S(1)} fusion(f32[4,2,16,1152]{3,2,1,0:T(8,128)S(1)} %all_gather.15, f32[4,540,1152,1]{2,0,1,3:T(4,128)} %bitcast.77, f32[4,2,540]{2,1,0:T(2,128)S(1)} %pad_maximum_fusion.1), kind=kOutput, calls=%fused_computation.28 | convolution fusion | flops 955584000 | bytes 10836864 | tf_op jit(solution)/shard_map/scnr,slr->scnl/dot_general | solution.py:43
  96.8 3.5 fusion.26
  102.8 13.1 %fusion.15 = f32[4,2,16,1152]{3,2,1,0:T(8,128)} fusion(f32[4,540,1152,1]{2,0,1,3:T(4,128)} %bitcast.78, f32[4,2,16,540]{3,2,1,0:T(8,128)S(1)} %reshape.291, f32[4,2,540]{2,1,0:T(2,128)S(1)} %pad_maximum_fusion.1), kind=kOutput, calls=%fused_computation.15 | convolution fusion | flops 955584000 | bytes 10836864 | tf_op jit(solution)/shard_map/scnl,slr->scnr/dot_general | solution.py:39
  115.9 21.1 %reduce-scatter.8.cloned.1.call-done = f32[1,2,16,1152]{3,2,1,0:T(8,128)} async-done(((f32[4,2,16,1152]{3,2,1,0:T(8,128)}), f32[1,2,16,1152]{3,2,1,0:T(8,128)}) %reduce-scatter.8.cloned.1.call-update) | async-done | bytes 147472 | tf_op jit(solution)/shard_map/reduce_scatter | solution.py:107
  137.0 2.2 copy.63
  139.2 3.6 reshape.314
  142.8 5.5 all-to-all-start.1
  150.3 1.9 reshape.306
  152.1 3.7 all-to-all-done.1
  156.4 2.6 reduce
  159.0 3.5 reshape.315
  162.5 2.3 copy.64
  164.8 10.7 %all-gather = f32[32,1,2,16,144]{4,3,2,1,0:T(8,128)} all-gather(f32[8,1,2,16,144]{4,3,2,1,0:T(8,128)} %bitcast.89), channel_id=2, replica_groups=mesh['blk'=8,'lon'=4] {'lon'}, dimensions={0}, use_global_device_ids=true | all-gather | bytes 737280 | tf_op jit(solution)/shard_map/all_gather | solution.py:111
  175.5 2.6 reshape.292
  178.0 2.8 dot_general.49
  180.9 10.7 %fusion.49 = f32[16,144,1080]{2,1,0:T(8,128)S(1)} fusion(f32[64,1080,1]{1,0,2:T(8,128)} %reshape.306, f32[16,144,64]{1,0,2:T(8,128)} %dot_general.49), kind=kOutput, calls=%fused_computation.35 | convolution fusion | flops 1911029760 | bytes 10819584 | tf_op jit(solution)/shard_map/dot_general | solution.py:112
  191.6 13.6 %fusion.2 = f32[32,2,16,144]{3,0,2,1:T(8,128)} fusion(f32[16,144,1080]{2,1,0:T(8,128)S(1)} %fusion.49, f32[144,1080]{1,0:T(8,128)S(1)} %select_add_fusion, f32[32,1,1080]{2,0,1:T(8,128)S(1)} %copy-done.6, f32[32,1,1080]{2,0,1:T(8,128)S(1)} %copy-done.3), kind=kOutput, calls=%fused_computation.2 | convolution fusion | flops 1913587200 | bytes 11441664 | tf_op jit(solution)/shard_map/dot_general | solution.py:76
  205.2 23.3 %reduce-scatter.10.cloned.1.call-done = f32[8,2,16,144]{3,0,2,1:T(8,128)} async-done(((f32[32,2,16,144]{3,0,2,1:T(8,128)}), f32[8,2,16,144]{3,0,2,1:T(8,128)}) %reduce-scatter.10.cloned.1.call-update) | async-done | bytes 147472 | tf_op jit(solution)/shard_map/reduce_scatter | solution.py:77
  229.5 14.1 %all_to_all.90 = f32[8,2,16,144]{3,2,1,0:T(8,128)S(1)} all-to-all(f32[8,2,16,144]{3,2,1,0:T(8,128)S(1)} %copy.67), channel_id=1, replica_groups=mesh['blk'=8,'lon'=4] {'blk'}, dimensions={0} | all-to-all | bytes 294912 | tf_op jit(solution)/shard_map/all_to_all | solution.py:83
  246.2 7.3 %all_gather.17 = f32[4,2,16,1152]{3,2,1,0:T(8,128)S(1)} all-gather(f32[1,2,16,1152]{3,2,1,0:T(8,128)} %all_to_all.76), channel_id=1, replica_groups=mesh['blk'=8,'lon'=4] {'lon'}, dimensions={0}, use_global_device_ids=true | all-gather | bytes 737280 | tf_op jit(solution)/shard_map/all_gather | solution.py:84
  253.5 14.3 %multiply_reduce_fusion.2 = (f32[16]{0:T(128)}, f32[16]{0:T(128)}, f32[4,2,16,540]{3,2,1,0:T(8,128)}) fusion(f32[4,2,16,540]{3,2,1,0:T(8,128)S(1)} %reshape.291, f32[4,2,540]{2,1,0:T(2,128)S(1)} %pad_maximum_fusion.1, f32[4,2,16,540]{3,2,1,0:T(8,128)S(1)} %fusion.32, f32[540]{0:T(1024)S(1)} %copy-done.9, f32[4,2,16,1152]{3,2,1,0:T(8,128)S(1)} %all_gather.17, ...), kind=kOutput, calls=%fused_computation.46 | convolution fusion | flops 956067840 | bytes 11392112 | tf_op jit(solution)/shard_map/scnr,slr->scnl/dot_general | solution.py:43
  267.8 39.0 %all-reduce = (f32[16]{0:T(128)}, f32[16]{0:T(128)}) all-reduce(f32[16]{0:T(128)} %get-tuple-element.3, f32[16]{0:T(128)} %get-tuple-element.2), channel_id=1, replica_groups=mesh['blk'=8,'lon'=4] {'blk','lon'}, use_global_device_ids=true, to_apply=%region_2.3 | all-reduce | flops 32 | bytes 256 | tf_op jit(solution)/shard_map/psum | solution.py:98
  309.8 2.2 reshape.294
  312.0 3.5 fusion.29
  319.8 40.9 %psum.30 = f32[16]{0:T(128)} all-reduce(f32[16]{0:T(128)} %multiply_reduce_fusion.1), channel_id=1, replica_groups=mesh['blk'=8,'lon'=4] {'blk','lon'}, use_global_device_ids=true, to_apply=%region_8.9 | all-reduce | flops 16 | bytes 128 | tf_op jit(solution)/shard_map/psum | solution.py:98
  362.5 13.1 %fusion.11 = f32[4,2,16,1152]{3,2,1,0:T(8,128)} fusion(f32[4,2,16,540]{3,2,1,0:T(8,128)S(1)} %multiply_add_fusion.1, f32[4,540,1152,1]{2,0,1,3:T(4,128)} %bitcast.80), kind=kOutput, calls=%fused_computation.11 | convolution fusion | flops 955514880 | bytes 10819584 | tf_op jit(solution)/shard_map/scnl,slr->scnr/dot_general | solution.py:39
  375.7 22.2 %reduce-scatter.12.cloned.1.call-done = f32[1,2,16,1152]{3,2,1,0:T(8,128)} async-done(((f32[4,2,16,1152]{3,2,1,0:T(8,128)}), f32[1,2,16,1152]{3,2,1,0:T(8,128)}) %reduce-scatter.12.cloned.1.call-update) | async-done | bytes 147472 | tf_op jit(solution)/shard_map/reduce_scatter | solution.py:107
  397.9 2.2 copy.74
  400.1 3.6 reshape.316
  403.7 13.1 %all_to_all.91 = f32[8,1,4608]{2,1,0:T(1,128)} all-to-all(f32[8,1,4608]{2,1,0:T(1,128)} %reshape.316), channel_id=1, replica_groups=mesh['blk'=8,'lon'=4] {'blk'}, dimensions={0} | all-to-all | bytes 294912 | tf_op jit(solution)/shard_map/all_to_all | solution.py:110
  416.8 2.6 reduce.1
  419.3 3.5 reshape.317
  422.8 2.3 copy.75
  425.1 10.7 %all-gather.1 = f32[32,1,2,16,144]{4,3,2,1,0:T(8,128)} all-gather(f32[8,1,2,16,144]{4,3,2,1,0:T(8,128)} %bitcast.91), channel_id=3, replica_groups=mesh['blk'=8,'lon'=4] {'lon'}, dimensions={0}, use_global_device_ids=true | all-gather | bytes 737280 | tf_op jit(solution)/shard_map/all_gather | solution.py:111
  435.8 2.6 reshape.296
  438.4 2.8 dot_general.56
  441.2 10.7 %fusion.47 = f32[16,144,1080]{2,1,0:T(8,128)S(1)} fusion(f32[64,1080,1]{1,0,2:T(8,128)} %reshape.306, f32[16,144,64]{1,0,2:T(8,128)} %dot_general.56), kind=kOutput, calls=%fused_computation.33 | convolution fusion | flops 1911029760 | bytes 10819584 | tf_op jit(solution)/shard_map/dot_general | solution.py:112
  451.9 13.6 %fusion = f32[32,2,16,144]{3,0,2,1:T(8,128)} fusion(f32[16,144,1080]{2,1,0:T(8,128)S(1)} %fusion.47, f32[144,1080]{1,0:T(8,128)S(1)} %select_add_fusion, f32[32,1,1080]{2,0,1:T(8,128)S(1)} %copy-done.7, f32[32,1,1080]{2,0,1:T(8,128)S(1)} %copy-done.4), kind=kOutput, calls=%fused_computation | convolution fusion | flops 1913587200 | bytes 11441664 | tf_op jit(solution)/shard_map/dot_general | solution.py:76
  465.6 23.0 %reduce-scatter.14.cloned.1.call-done = f32[8,2,16,144]{3,0,2,1:T(8,128)} async-done(((f32[32,2,16,144]{3,0,2,1:T(8,128)}), f32[8,2,16,144]{3,0,2,1:T(8,128)}) %reduce-scatter.14.cloned.1.call-update) | async-done | bytes 147472 | tf_op jit(solution)/shard_map/reduce_scatter | solution.py:77
  489.6 14.1 %all_to_all.92 = f32[8,2,16,144]{3,2,1,0:T(8,128)S(1)} all-to-all(f32[8,2,16,144]{3,2,1,0:T(8,128)S(1)} %copy.77), channel_id=1, replica_groups=mesh['blk'=8,'lon'=4] {'blk'}, dimensions={0} | all-to-all | bytes 294912 | tf_op jit(solution)/shard_map/all_to_all | solution.py:83
  504.6 6.9 %all_gather.19 = f32[4,2,16,1152]{3,2,1,0:T(8,128)S(1)} all-gather(f32[1,2,16,1152]{3,2,1,0:T(8,128)} %all_to_all.84), channel_id=1, replica_groups=mesh['blk'=8,'lon'=4] {'lon'}, dimensions={0}, use_global_device_ids=true | all-gather | bytes 737280 | tf_op jit(solution)/shard_map/all_gather | solution.py:84
  511.5 16.9 %multiply_reduce_fusion = (f32[16]{0:T(128)S(1)}, f32[4,2,16,540]{3,2,1,0:T(8,128)S(1)}) fusion(f32[4,2,16,540]{3,2,1,0:T(8,128)S(1)} %multiply_add_fusion.1, f32[540]{0:T(1024)S(1)} %copy-done.9, f32[4,2,16,1152]{3,2,1,0:T(8,128)S(1)} %all_gather.19, f32[4,540,1152,1]{2,0,1,3:T(4,128)} %bitcast.81, f32[4,2,540]{2,1,0:T(2,128)S(1)} %pad_maximum_fusion.1), kind=kOutput, calls=%fused_computation.42 | convolution fusion | flops 955860480 | bytes 11115568 | tf_op jit(solution)/shard_map/scnr,slr->scnl/dot_general | solution.py:43
  528.4 38.7 %psum.31 = f32[16]{0:T(128)S(1)} all-reduce(f32[16]{0:T(128)S(1)} %get-tuple-element.13), channel_id=1, replica_groups=mesh['blk'=8,'lon'=4] {'blk','lon'}, use_global_device_ids=true, to_apply=%region_12.13 | all-reduce | flops 16 | bytes 128 | tf_op jit(solution)/shard_map/psum | solution.py:119
  (70 shorter events, 30.0 us)
Async XLA Ops:
  7.2 89.6 %copy-start = (f32[4,4,135,135]{3,1,2,0:T(4,128)S(1)}, f32[4,4,135,135]{3,1,2,0:T(4,128)}, u32[]{:S(2)}) copy-start(f32[4,4,135,135]{3,1,2,0:T(4,128)} %param.9) | copy-start | bytes 3499204
  7.2 46.6 %reduce-scatter.6.cloned.1.call-start = ((), (), s32[]{:S(2)}) async-start(), calls=%async_computation.10 | async-start | bytes 1310720 | tf_op jit(solution)/shard_map/reduce_scatter | solution.py:77
  10.3 85.3 %copy-start.2 = (f32[32,1,1080]{2,0,1:T(8,128)}, f32[32,1,1080]{2,0,1:T(8,128)S(1)}, u32[]{:S(2)}) copy-start(f32[32,1,1080]{2,0,1:T(8,128)S(1)} %get-tuple-element.8) | copy-start | bytes 414724
  10.3 85.3 %copy-start.5 = (f32[32,1,1080]{2,0,1:T(8,128)}, f32[32,1,1080]{2,0,1:T(8,128)S(1)}, u32[]{:S(2)}) copy-start(f32[32,1,1080]{2,0,1:T(8,128)S(1)} %get-tuple-element.9) | copy-start | bytes 414724
  55.5 14.3 %all-to-all-start = ((f32[8,2,16,144]{3,2,1,0:T(8,128)}), f32[8,2,16,144]{3,2,1,0:T(8,128)S(1)}, u32[]{:S(2)}, u32[]{:S(2)}) async-start(f32[8,2,16,144]{3,2,1,0:T(8,128)} %copy.56), calls=%async_computation.1 | async-start | bytes 524288 | tf_op jit(solution)/shard_map/all_to_all | solution.py:83
  61.0 76.1 %reduce-scatter.8.cloned.1.call-start = ((), (), s32[]{:S(2)}) async-start(), calls=%async_computation.11 | async-start | bytes 737280 | tf_op jit(solution)/shard_map/reduce_scatter | solution.py:107
  142.8 13.1 %all-to-all-start.1 = ((f32[8,1,4608]{2,1,0:T(1,128)}), f32[8,1,4608]{2,1,0:T(1,128)}, u32[]{:S(2)}, u32[]{:S(2)}) async-start(f32[8,1,4608]{2,1,0:T(1,128)} %reshape.314), calls=%async_computation.3 | async-start | bytes 294912 | tf_op jit(solution)/shard_map/all_to_all | solution.py:110
  148.3 80.2 %reduce-scatter.10.cloned.1.call-start = ((), (), s32[]{:S(2)}) async-start(), calls=%async_computation.12 | async-start | bytes 1310720 | tf_op jit(solution)/shard_map/reduce_scatter | solution.py:77
  180.9 10.7 %copy-start.3 = (f32[32,1,1080]{2,0,1:T(8,128)S(1)}, f32[32,1,1080]{2,0,1:T(8,128)}, u32[]{:S(2)}) copy-start(f32[32,1,1080]{2,0,1:T(8,128)} %copy-done.2) | copy-start | bytes 414724
  180.9 10.7 %copy-start.6 = (f32[32,1,1080]{2,0,1:T(8,128)S(1)}, f32[32,1,1080]{2,0,1:T(8,128)}, u32[]{:S(2)}) copy-start(f32[32,1,1080]{2,0,1:T(8,128)} %copy-done.5) | copy-start | bytes 414724
  191.6 61.9 %copy-start.9 = (f32[540]{0:T(1024)S(1)}, f32[540]{0:T(1024)}, u32[]{:S(2)}) copy-start(f32[540]{0:T(1024)} %param.10) | copy-start | bytes 6484
  205.2 192.8 %reduce-scatter.12.cloned.1.call-start = ((), (), s32[]{:S(2)}) async-start(), calls=%async_computation.13 | async-start | bytes 737280 | tf_op jit(solution)/shard_map/reduce_scatter | solution.py:107
  307.4 0.6 copy-start.10
  318.0 42.8 %copy-start.8 = (f32[4,2,16,540]{3,2,1,0:T(8,128)}, f32[4,2,16,540]{3,2,1,0:T(8,128)S(1)}, u32[]{:S(2)}) copy-start(f32[4,2,16,540]{3,2,1,0:T(8,128)S(1)} %reshape.295) | copy-start | bytes 829444
  375.7 112.8 %reduce-scatter.14.cloned.1.call-start = ((), (), s32[]{:S(2)}) async-start(), calls=%async_computation.14 | async-start | bytes 1310720 | tf_op jit(solution)/shard_map/reduce_scatter | solution.py:77
  441.2 10.7 %copy-start.4 = (f32[32,1,1080]{2,0,1:T(8,128)S(1)}, f32[32,1,1080]{2,0,1:T(8,128)}, u32[]{:S(2)}) copy-start(f32[32,1,1080]{2,0,1:T(8,128)} %copy-done.2) | copy-start | bytes 414724
  441.2 10.7 %copy-start.7 = (f32[32,1,1080]{2,0,1:T(8,128)S(1)}, f32[32,1,1080]{2,0,1:T(8,128)}, u32[]{:S(2)}) copy-start(f32[32,1,1080]{2,0,1:T(8,128)} %copy-done.5) | copy-start | bytes 414724
  465.5 102.2 %copy-start.1 = (f32[4,2,16,540]{3,2,1,0:T(8,128)S(1)}, f32[4,2,16,540]{3,2,1,0:T(8,128)}, u32[]{:S(2)}) copy-start(f32[4,2,16,540]{3,2,1,0:T(8,128)} %multiply_subtract_fusion.1) | copy-start | bytes 829444
  465.5 102.2 %copy-start.11 = (f32[16]{0:T(128)S(1)}, f32[16]{0:T(128)}, u32[]{:S(2)}) copy-start(f32[16]{0:T(128)} %copy-done.10) | copy-start | bytes 196
Sparse Core Ops, SparseCore 0:
  26.2 27.4 reduce-scatter.5
  116.1 20.9 reduce-scatter.7
  205.3 23.1 reduce-scatter.9
  375.8 22.1 reduce-scatter.11
  465.7 22.7 reduce-scatter.13
where the time goes:
time: 582 us; the launch traced here: 576 us
  blocking collectives  202 us (35%)
  matrix products  146 us (25%)
  waiting for transfers between devices  129 us (22%)
  local copies, waits for them, and re-layouts  55.7 us (10%)
  other arithmetic  16.9 us (3%)
  between operations  14.4 us (2%)
  starting transfers between devices  11.2 us (2%)
    psum x2, blocking collectives, fit_sum(): return lax.psum(column_dot(lhs_values, rhs_values), ('blk', 'lon'))  79.9 us
    reduce_scatter x3, waiting for transfers between devices, analyse(): lax.psum_scatter(product.reshape(window // lon_count * lax.axis_size('lon...  73.7 us
    dot_general x3, matrix products, legendre_down(): jnp.einsum('scnr,slr->scnl', cycles_part, basis_rows, precision=HIGHEST)  48.3 us
    reduce_scatter x2, waiting for transfers between devices, body(): lax.psum_scatter(legendre_up(synthesize_coeffs, legendre), 'lon', scatter...  43.3 us
    dot_general x3, matrix products, analyse(): lax.dot_general(trig_rows, flat_grid, (((1,), (1,)), ((), ())), precision...  42.9 us
    psum x1, blocking collectives, body(): curvature_sum = lax.psum(column_dot(direction, image_vec), ('blk', 'lon'))  38.7 us
    all_to_all x2, blocking collectives, analyse(): lax.all_to_all(shared, 'blk', split_axis=0, concat_axis=3, tiled=True)  28.1 us
    dot_general x2, matrix products, legendre_up(): return jnp.einsum('scnl,slr->scnr', coeffs, basis_rows, precision=HIGHEST)  26.2 us
  transfers between devices with their start and end apart: 7, of which 7 were waited for; matrix products, arithmetic and copies ran while one was open for 1% of the time, Pallas kernels for 0%

commit v1 on v0

--- a/solution.py
+++ b/solution.py
@@ -1,8 +1,11 @@
+import functools
 import math
 
 import jax
 import jax.numpy as jnp
 from jax import lax
+from jax.experimental import pallas as pl
+from jax.experimental.pallas import tpu as pltpu
 from jax.sharding import PartitionSpec as P
 
 ITERS = 2
@@ -10,6 +13,9 @@
 
 HUBER_LEVELS = (1.0, 0.5, 0.25, 0.125)
 HIGHEST = lax.Precision.HIGHEST
+GROUP = 8
+MESH = pl.DeviceIdType.MESH
+VMEM_WHOLE = pl.BlockSpec(memory_space=pltpu.VMEM)
 
 
 def build_mask(orders, first_degree, degrees):
@@ -43,7 +49,7 @@
     return jnp.einsum("scnr,slr->scnl", cycles_part, basis_rows, precision=HIGHEST)
 
 
-def body(anomalies, classes, legendre, precond, prior, assign):
+def plain_body(anomalies, classes, legendre, precond, prior, assign):
     lon_count = lax.axis_size("lon")
     blk_count = lax.axis_size("blk")
     blk_place = lax.axis_index("blk")
@@ -128,6 +134,462 @@
     return (solution, residual)
 
 
+def split(values):
+    high = values.astype(jnp.bfloat16)
+    return high, (values - high.astype(jnp.float32)).astype(jnp.bfloat16)
+
+
+def split_outside(values):
+    high = lax.reduce_precision(values, 8, 7)
+    return high.astype(jnp.bfloat16), (values - high).astype(jnp.bfloat16)
+
+
+def exchange_kernel(
+    blocks, p_ref, o_ref, from_core, summed, from_x, ready, send_sem, recv_sem
+):
+    blk = lax.axis_index("blk")
+    lon = lax.axis_index("lon")
+    core, x = lon % 2, lon // 2
+    core_mate = (blk, lon + 1 - 2 * core)
+    x_mate = (blk, lon + 2 - 4 * x)
+    part = from_x.shape[1]
+    mine = pl.ds(pl.multiple_of(part * x, 8), part)
+    theirs = pl.ds(pl.multiple_of(part * (1 - x), 8), part)
+    barrier = pltpu.get_barrier_semaphore()
+    peers = [core_mate, x_mate] + [((blk + j) % blocks, lon) for j in range(1, blocks)]
+    for peer in peers:
+        pl.semaphore_signal(barrier, inc=1, device_id=peer, device_id_type=MESH)
+    pl.semaphore_wait(barrier, len(peers))
+
+    def copy(stage, j, src, dst, peer):
+        return pltpu.make_async_remote_copy(
+            src_ref=src,
+            dst_ref=dst,
+            send_sem=send_sem.at[stage, j],
+            recv_sem=recv_sem.at[stage, j],
+            device_id=peer,
+            device_id_type=MESH,
+        )
+
+    order = sorted(range(blocks), key=lambda j: (j == 0, abs(j - blocks // 2)))
+    started = {}
+
+    def launch(stage, j, src, dst, peer):
+        started[stage, j] = copy(stage, j, src, dst, peer)
+        started[stage, j].start()
+
+    for j in order:
+        to = (blk + j) % blocks
+        launch(0, j, p_ref.at[to, 1 - core], from_core.at[to], core_mate)
+
+    def over_x(j):
+        to = (blk + j) % blocks
+        started[0, j].wait_recv()
+        summed[to] = p_ref[to, core] + from_core[to]
+        launch(1, j, summed.at[to, theirs], from_x.at[to], x_mate)
+
+    def over_blk(j):
+        to = (blk + j) % blocks
+        started[1, j].wait_recv()
+        value = summed[to, mine] + from_x[to]
+        if j == 0:
+            o_ref[blk, core, mine] = value
+        else:
+            ready[to] = value
+            launch(2, j, ready.at[to], o_ref.at[blk, core, mine], (to, lon))
+
+    for step in range(blocks + 2):
+        if step < blocks:
+            over_x(order[step])
+        if step >= 2:
+            over_blk(order[step - 2])
+    arrivals = order[-1:] + order[:-1]
+    for j in arrivals:
+        source = (blk - j + blocks) % blocks
+        if j:
+            started[2, j].wait_recv()
+        held = o_ref.at[source, core, mine]
+        launch(3, j, held, held, x_mate)
+        launch(4, j, held, held, core_mate)
+    for j in arrivals:
+        source = (blk - j + blocks) % blocks
+        started[3, j].wait_recv()
+        held = o_ref.at[source, core, theirs]
+        launch(5, j, held, held, core_mate)
+    for j in arrivals:
+        started[4, j].wait_recv()
+        started[5, j].wait_recv()
+    for one in started.values():
+        one.wait_send()
+
+
+def exchange(partial):
+    blocks, halves, padded, lanes = partial.shape
+    return pl.pallas_call(
+        functools.partial(exchange_kernel, blocks),
+        out_shape=jax.ShapeDtypeStruct(partial.shape, jnp.float32),
+        in_specs=[VMEM_WHOLE],
+        out_specs=VMEM_WHOLE,
+        scratch_shapes=[
+            pltpu.VMEM((blocks, padded, lanes), jnp.float32),
+            pltpu.VMEM((blocks, padded, lanes), jnp.float32),
+            pltpu.VMEM((blocks, padded // 2, lanes), jnp.float32),
+            pltpu.VMEM((blocks, padded // 2, lanes), jnp.float32),
+            pltpu.SemaphoreType.DMA((6, blocks)),
+            pltpu.SemaphoreType.DMA((6, blocks)),
+        ],
+        compiler_params=pltpu.CompilerParams(collective_id=0, has_side_effects=True),
+        name="exchange",
+    )(partial)
+
+
+def group_sum(tile, group):
+    lanes = tile.shape[1]
+    at = lax.broadcasted_iota(jnp.int32, tile.shape, 1)
+    shift = 1
+    while shift < group:
+        ahead = pltpu.roll(tile, lanes - shift, 1)
+        behind = pltpu.roll(tile, shift, 1)
+        tile = tile + jnp.where(at // shift % 2 == 0, ahead, behind)
+        shift *= 2
+    return tile
+
+
+def sums_of(o_ref, half, group):
+    tile = o_ref[0, 0, half:half + 8]
+    for b in range(1, o_ref.shape[0]):
+        tile = tile + o_ref[b, 0, half:half + 8]
+    return group_sum(tile, group)
+
+
+def pick_row(tile, row):
+    return tile[row:row + 1]
+
+
+def tile_of(rows):
+    lanes = rows[0].shape[1]
+    at = lax.broadcasted_iota(jnp.int32, (8, lanes), 0)
+    tile = jnp.zeros((8, lanes), jnp.float32)
+    for index, row in enumerate(rows):
+        tile = jnp.where(at == index, jnp.broadcast_to(row, (8, lanes)), tile)
+    return tile
+
+
+def grid_kernel(kind, half, *refs):
+    columns = pl.num_programs(0)
+    n = pl.program_id(0)
+    if kind == "data":
+        field, weights, trig_down, trig_low, p_ref, down = refs
+    elif kind == "first":
+        o_ref, weights, trig_up, trig_down, trig_low, p_ref, q_ref, down, up, cycles = refs
+    else:
+        (o_ref, old_ref, old_q, weights, trig_up, trig_down, trig_low,
+         p_ref, q_ref, down, up, cycles) = refs
+    blocks, lanes = down.shape[0], down.shape[1]
+    group = GROUP
+    if kind != "data":
+        @pl.when(n == 0)
+        def _():
+            sums = sums_of(o_ref, half, group)
+            if kind == "first":
+                q_ref[...] = sums
+            else:
+                before = old_q[...]
+                beta = pick_row(sums, 0) / pick_row(before, 0)
+                norm = (
+                    pick_row(sums, 1)
+                    + 2.0 * beta * pick_row(sums, 2)
+                    + beta * beta * pick_row(before, 1)
+                )
+                q_ref[...] = tile_of([pick_row(sums, 0), norm, beta])
+            for b in range(blocks):
+                for h in range(2):
+                    rows = o_ref[b, h, 0:half]
+                    if kind != "first":
+                        rows = rows + beta * old_ref[b, h, 0:half]
+                    cycles[b, h * half:(h + 1) * half] = rows
+                up[b] = cycles[b].T
+
+        stack = jnp.concatenate(
+            [up[b, pl.ds(pl.multiple_of(n * group, 8), group), :] for b in range(blocks)], axis=0
+        )
+        high = stack.astype(jnp.bfloat16).astype(jnp.float32)
+        triple = jnp.concatenate([high, high, stack - high], axis=0).T.astype(jnp.bfloat16)
+        grid_field = jnp.dot(triple, trig_up[...], preferred_element_type=jnp.float32)
+    else:
+        grid_field = field[0]
+    high, low = split(grid_field * weights[...])
+    sums = jnp.dot(high, trig_down[...], preferred_element_type=jnp.float32)
+    sums = sums + jnp.dot(low, trig_low[...], preferred_element_type=jnp.float32)
+    sums = sums.T
+    sums = sums[: 8 * blocks] + sums[8 * blocks:]
+    for b in range(blocks):
+        down[b, pl.ds(pl.multiple_of(n * group, 8), group), :] = sums[8 * b:8 * b + 8]
+
+    @pl.when(n == columns - 1)
+    def _():
+        total = jnp.zeros((1, lanes), jnp.float32)
+        for b in range(blocks):
+            rows = down[b].T
+            if kind != "data":
+                total = total + jnp.sum(rows * cycles[b], axis=0, keepdims=True)
+            for h in range(2):
+                p_ref[b, h, 0:half] = rows[h * half:(h + 1) * half]
+        for b in range(blocks):
+            for h in range(2):
+                p_ref[b, h, half:] = jnp.zeros((p_ref.shape[2] - half, lanes), jnp.float32)
+            if kind != "data":
+                p_ref[b, 0, half:half + 8] = tile_of([total])
+
+
+def grid_call(kind, blocks, lanes, cycle_count, rhs_count, *operands):
+    half = cycle_count // 2
+    padded = -(-(half + 8) // 16) * 16
+    out_shape = [jax.ShapeDtypeStruct((blocks, 2, padded, lanes), jnp.float32)]
+    scratch = [pltpu.VMEM((blocks, lanes, cycle_count), jnp.float32)]
+    in_specs = [VMEM_WHOLE] * len(operands)
+    if kind == "data":
+        in_specs[0] = pl.BlockSpec((1,) + operands[0].shape[1:], lambda n: (n, 0, 0))
+    else:
+        out_shape.append(jax.ShapeDtypeStruct((8, lanes), jnp.float32))
+        scratch.append(pltpu.VMEM((blocks, lanes, cycle_count), jnp.float32))
+        scratch.append(pltpu.VMEM((blocks, cycle_count, lanes), jnp.float32))
+    return pl.pallas_call(
+        functools.partial(grid_kernel, kind, half),
+        grid=(rhs_count,),
+        out_shape=out_shape,
+        in_specs=in_specs,
+        out_specs=[VMEM_WHOLE] * len(out_shape),
+        scratch_shapes=scratch,
+        compiler_params=pltpu.CompilerParams(vmem_limit_bytes=60 << 20),
+        name="grid_" + kind,
+    )(*operands)
+
+
+def to_column(row):
+    return jnp.broadcast_to(row, (row.shape[1], row.shape[1])).T
+
+
+def product(lhs, high, low, dims):
+    lhs_high, lhs_low = split(lhs)
+    rows = lhs.shape[0]
+    both = jnp.concatenate([lhs_high, lhs_low], axis=0)
+    first = lax.dot_general(both, high, dims, preferred_element_type=jnp.float32)
+    second = lax.dot_general(lhs_high, low, dims, preferred_element_type=jnp.float32)
+    return first[:rows] + first[rows:] + second
+
+
+NN = (((1,), (0,)), ((), ()))
+NT = (((1,), (1,)), ((), ()))
+
+
+def coeff_kernel(kind, half, *refs):
+    s = pl.program_id(0)
+    if kind == "first":
+        (o_ref, leg_high, leg_low, pre_high, pre_low, live, prior,
+         p_ref, residual, z_out, spread_down, turned_down, tiles, up, dots) = refs
+    elif kind == "middle":
+        (o_ref, q_ref, leg_high, leg_low, pre_high, pre_low, live, prior, old, direction,
+         p_ref, residual, z_out, solution, spread_down, turned_down, tiles, up, dots, alphas) = refs
+    else:
+        (o_ref, q_ref, leg_high, leg_low, live, prior, old, direction, z_in, old_solution,
+         residual, solution, spread_down, turned_down, tiles, alphas) = refs
+    blocks = o_ref.shape[0]
+    lanes = o_ref.shape[3]
+    group = GROUP
+    rows = residual.shape[1]
+
+    @pl.when(s == 0)
+    def _():
+        for b in range(blocks):
+            for h in range(2):
+                spread_down[(2 * b + h) * half:(2 * b + h + 1) * half, :] = o_ref[b, h, 0:half]
+        for k in range(tiles.shape[0]):
+            tiles[k] = spread_down[k * lanes:(k + 1) * lanes, :].T
+            for piece in range(group):
+                turned_down[piece * rows // 2:(piece + 1) * rows // 2, k * lanes:(k + 1) * lanes] = tiles[
+                    k, pl.ds(piece, rows // 2, stride=group), :
+                ]
+        if kind != "first":
+            sums = sums_of(o_ref, half, group)
+            scalars = q_ref[...]
+            alpha = pick_row(scalars, 0) / (pick_row(sums, 0) + pick_row(scalars, 1))
+            wanted = [alpha, pick_row(scalars, 2)] if kind == "last" else [alpha]
+            for index, row in enumerate(wanted):
+                tiles[0] = to_column(row)
+                once = tiles[0, pl.ds(0, rows // 2, stride=group), :]
+                alphas[index] = jnp.concatenate([once, once], axis=0)
+
+    where = pl.ds(pl.multiple_of(s * rows, rows), rows)
+    cycles = turned_down[where, :]
+    image = product(cycles, leg_high[0], leg_low[0], NT)
+    mask = live[0]
+    if kind == "first":
+        res = mask * image
+    else:
+        alpha = alphas[0, :, 0:1]
+        d = direction[0]
+        if kind == "last":
+            d = z_in[0] + alphas[1, :, 0:1] * d
+        image = mask * (image + prior[...] * d)
+        res = old[0] - alpha * image
+        if kind == "last":
+            solution[0] = old_solution[0] + alpha * d
+        else:
+            solution[0] = alpha * d
+    residual[0] = res
+    if kind == "last":
+        return
+    z = mask * product(res, pre_high[0], pre_low[0], NN)
+    z_out[0] = z
+    pairs = [res * z, prior[...] * z * z]
+    if kind == "middle":
+        pairs.append(prior[...] * z * d)
+    for index, pair in enumerate(pairs):
+        dots[index, where, :] = jnp.broadcast_to(
+            jnp.sum(pair, axis=1, keepdims=True), (rows, lanes)
+        )
+    up[where, :] = product(z, leg_high[0], leg_low[0], NN)
+
+    @pl.when(s == pl.num_programs(0) - 1)
+    def _():
+        sums = []
+        for index in range(len(pairs)):
+            column = dots[index, 0:rows // 2]
+            for piece in range(1, group):
+                column = column + dots[index, piece * rows // 2:(piece + 1) * rows // 2]
+            tiles[0] = jnp.zeros((lanes, lanes), jnp.float32)
+            tiles[0, pl.ds(0, rows // 2, stride=group), :] = column
+            sums.append(tiles[0].T[0:1])
+        tile = tile_of(sums)
+        for k in range(tiles.shape[0]):
+            for piece in range(group):
+                tiles[k, pl.ds(piece, rows // 2, stride=group), :] = up[
+                    piece * rows // 2:(piece + 1) * rows // 2, k * lanes:(k + 1) * lanes
+                ]
+            spread_down[k * lanes:(k + 1) * lanes, :] = tiles[k].T
+        for b in range(blocks):
+            for h in range(2):
+                at = (2 * b + h) * half
+                p_ref[b, h, 0:half] = spread_down[at:at + half, :]
+                p_ref[b, h, half:] = jnp.zeros((p_ref.shape[2] - half, lanes), jnp.float32)
+            p_ref[b, 0, half:half + 8] = tile
+
+
+def coeff_call(kind, cycle_count, lanes, *operands):
+    legendre_at = 1 if kind == "first" else 2
+    slots, degrees, cycles = operands[legendre_at].shape
+    rows = lanes // slots
+    blocks, _, padded, _ = operands[0].shape
+    in_specs = []
+    for place, operand in enumerate(operands):
+        if place >= legendre_at and operand.ndim == 3:
+            in_specs.append(pl.BlockSpec((1,) + operand.shape[1:], lambda s: (s, 0, 0)))
+        else:
+            in_specs.append(VMEM_WHOLE)
+    vector = jax.ShapeDtypeStruct((slots, rows, degrees), jnp.float32)
+    vector_spec = pl.BlockSpec((1, rows, degrees), lambda s: (s, 0, 0))
+    partial = jax.ShapeDtypeStruct(operands[0].shape, jnp.float32)
+    scratch = [
+        pltpu.VMEM((cycles, lanes), jnp.float32),
+        pltpu.VMEM((lanes, cycles), jnp.float32),
+        pltpu.VMEM((cycles // lanes, lanes, lanes), jnp.float32),
+    ]
+    if kind == "last":
+        out_shape, out_specs = [vector] * 2, [vector_spec] * 2
+    else:
+        vectors = 2 if kind == "first" else 3
+        out_shape = [partial] + [vector] * vectors
+        out_specs = [VMEM_WHOLE] + [vector_spec] * vectors
+        scratch.append(pltpu.VMEM((lanes, cycles), jnp.float32))
+        scratch.append(pltpu.VMEM((3, lanes, lanes), jnp.float32))
+    if kind != "first":
+        scratch.append(pltpu.VMEM((2, rows, lanes), jnp.float32))
+    return pl.pallas_call(
+        functools.partial(coeff_kernel, kind, cycle_count // 2),
+        grid=(slots,),
+        out_shape=out_shape,
+        in_specs=in_specs,
+        out_specs=out_specs,
+        scratch_shapes=scratch,
+        compiler_params=pltpu.CompilerParams(vmem_limit_bytes=60 << 20),
+        name="coeff_" + kind,
+    )(*operands)
+
+
+def fast_body(anomalies, classes, legendre, precond, prior, assign):
+    lon_count = lax.axis_size("lon")
+    blocks = lax.axis_size("blk")
+    blk_place = lax.axis_index("blk")
+    lon_place = lax.axis_index("lon")
+    slot_count, local_degrees, _ = legendre.shape
+    rhs_count, cycle_count, longitudes = anomalies.shape
+    window = assign.shape[0]
+    block_width = precond.shape[2]
+    lanes = slot_count * 2 * rhs_count
+    stride_value = local_degrees * lon_count // window
+    all_orders = assign * stride_value
+    own_orders = lax.dynamic_slice_in_dim(all_orders, blk_place * slot_count, slot_count)
+    live = build_mask(own_orders, lon_place * local_degrees, local_degrees)
+    live = jnp.broadcast_to(live, (slot_count, 2, rhs_count, local_degrees)).reshape(
+        slot_count, 2 * rhs_count, local_degrees
+    )
+    weights = huber_weights(classes)
+    trig = trig_table(
+        all_orders, lon_place * longitudes, longitudes, longitudes * lon_count
+    ).reshape(2 * window, longitudes)
+    trig_high, trig_rest = split_outside(trig)
+    trig_up = jnp.concatenate([trig_high, trig_rest, trig_high], axis=0)
+    trig_down = jnp.concatenate([trig_high, trig_rest], axis=0).T
+    trig_low = jnp.concatenate([trig_high, jnp.zeros_like(trig_high)], axis=0).T
+    leg = split_outside(legendre)
+    per_slot = precond.shape[1]
+    dense = precond[:, :, :, None, :] * jnp.eye(per_slot, dtype=jnp.float32)[None, :, None, :, None]
+    pre = split_outside(dense.reshape(slot_count, local_degrees, local_degrees))
+    prior_row = prior[None, :]
+    on_grid = functools.partial(grid_call)
+
+    sizes = (blocks, lanes, cycle_count, rhs_count)
+    (partial,) = on_grid("data", *sizes, anomalies, weights, trig_down, trig_low)
+    sums = exchange(partial)
+    partial, residual, direction = coeff_call(
+        "first", cycle_count, lanes, sums, *leg, *pre, live, prior_row
+    )
+    first_up = exchange(partial)
+    partial, scalars = on_grid(
+        "first", *sizes, first_up, weights, trig_up, trig_down, trig_low
+    )
+    sums = exchange(partial)
+    partial, residual, search, solved = coeff_call(
+        "middle", cycle_count, lanes, sums, scalars, *leg, *pre, live, prior_row,
+        residual, direction,
+    )
+    second_up = exchange(partial)
+    partial, scalars = on_grid(
+        "next", *sizes, second_up, first_up, scalars, weights, trig_up, trig_down, trig_low
+    )
+    sums = exchange(partial)
+    residual, solved = coeff_call(
+        "last", cycle_count, lanes, sums, scalars, *leg, live, prior_row,
+        residual, direction, search, solved,
+    )
+    shape = (slot_count, 2, rhs_count, local_degrees)
+    return solved.reshape(shape), residual.reshape(shape)
+
+
+def body(anomalies, classes, legendre, precond, prior, assign):
+    fits = (
+        lax.axis_size("lon") == 4
+        and lax.axis_size("blk") % 2 == 0
+        and anomalies.shape[1] % 16 == 0
+        and legendre.shape[0] * 2 == GROUP
+        and legendre.shape[2] % 128 == 0
+        and legendre.shape[0] * 2 * anomalies.shape[0] == 128
+    )
+    chosen = fast_body if fits else plain_body
+    return chosen(anomalies, classes, legendre, precond, prior, assign)
+
+
 def solution(mesh):
     in_specs = (
         P(None, "blk", "lon"),

time: 582 us -> 234 us (0.40)
  blocking collectives: 202 us -> 0 us
  Pallas kernels: 0 us -> 189 us
  matrix products: 146 us -> 0 us
  waiting for transfers between devices: 129 us -> 0 us
  local copies, waits for them, and re-layouts: 55.7 us -> 23.9 us
  between operations: 14.4 us -> 0.76 us
  starting transfers between devices: 11.2 us -> 0 us
    pallas_call x0 -> x11, Pallas kernels: none -> 189 us  [the longest x5 113 us: exchange(): pl.pallas_call(functools.partial(exchange_kernel, blocks), out_shape=jax....]
    dot_general x12 -> x0, matrix products: 146 us -> none  [the longest x3 48.3 us: legendre_down(): jnp.einsum('scnr,slr->scnl', cycles_part, basis_rows, precision=HIGHEST)]
    psum x3 -> x0, blocking collectives: 119 us -> none  [the longest x2 79.9 us: fit_sum(): return lax.psum(column_dot(lhs_values, rhs_values), ('blk', 'lon'))]
    reduce_scatter x5 -> x0, waiting for transfers between devices: 117 us -> none  [the longest x3 73.7 us: analyse(): lax.psum_scatter(product.reshape(window // lon_count * lax.axis_size('lon...]
    all_gather x5 -> x0, blocking collectives: 42.2 us -> none  [the longest x2 21.4 us: body(): lax.all_gather(moved, 'lon', axis=0, tiled=True).reshape(-1, grid_rows)]
    all_to_all x3 -> x0, blocking collectives: 41.2 us -> none  [the longest x2 28.1 us: analyse(): lax.all_to_all(shared, 'blk', split_axis=0, concat_axis=3, tiled=True)]
    mul x1 -> x4, local copies, waits for them, and re-layouts: 0.09 us -> 17.9 us  [fast_body(): precond[:, :, :, None, :]]
    convert_element_type x0 -> x4, other arithmetic: none -> 15.4 us  [the longest x3 15.4 us: split_outside(): return (high.astype(jnp.bfloat16), (values - high).astype(jnp.bfloat16))]
  transfers between devices with their start and end apart: 7 -> 0, of which waited for: 7 -> 0; matrix products, arithmetic and copies ran while one was open for 1% -> 0% of each run, Pallas kernels for 0% -> 0%
where the time goes in v1:
time: 234 us; the launch traced here: 233 us
  Pallas kernels  189 us (81%)
  local copies, waits for them, and re-layouts  23.9 us (10%)
  other arithmetic  19.4 us (8%)
    pallas_call x5, Pallas kernels, exchange(): pl.pallas_call(functools.partial(exchange_kernel, blocks), out_shape=jax....  113 us
    pallas_call x3, Pallas kernels, grid_call(): pl.pallas_call(functools.partial(grid_kernel, kind, half), grid=(rhs_coun...  44.1 us
    pallas_call x3, Pallas kernels, coeff_call(): pl.pallas_call(functools.partial(coeff_kernel, kind, cycle_count // 2), g...  31.9 us
    mul x4, local copies, waits for them, and re-layouts, fast_body(): precond[:, :, :, None, :]  17.9 us
    convert_element_type x3, other arithmetic, split_outside(): return (high.astype(jnp.bfloat16), (values - high).astype(jnp.bfloat16))  15.4 us

profile of v1, /device:TPU:0, one launch (start us, length us, event | category | flops | bytes accessed | tf_op | source)
XLA Modules:
  0.0 232.8 jit_solution(11590958951985359678)
XLA Ops:
  0.6 0.0 copy-start.1
  0.6 0.7 broadcast_multiply_fusion
  1.4 0.1 compare_convert_fusion.1
  1.5 1.3 broadcast_in_dim.5.refs_6_.refs_7_.refs_5_
  2.7 0.1 compare_select_fusion
  2.8 0.1 compare_convert_fusion
  2.9 0.7 fusion.7
  3.6 0.2 copy.20
  3.9 0.2 reshape.239
  4.1 0.2 copy.22
  4.3 0.2 copy.21
  4.5 0.1 fusion.10
  4.7 0.7 broadcast_in_dim.4
  5.4 0.3 pad_maximum_fusion
  5.7 1.0 copy.27.refs_2_.refs_4_
  6.7 1.0 pad_bitcast_fusion
  7.7 0.0 copy-done.1
  7.7 1.1 select_add_fusion.refs_1_.refs_3_
  8.7 14.7 %grid_data.1.p_ref = f32[8,2,80,128]{3,2,1,0:T(8,128)} custom-call(f32[16,144,1080]{2,1,0:T(8,128)} %refs_0_.1, f32[144,1080]{1,0:T(8,128)} %select_add_fusion.refs_1_.refs_3_, bf16[1080,128]{1,0:T(8,128)(2,1)} %get-tuple-element.37.refs_2_.refs_3_.refs_5_, bf16[1080,128]{1,0:T(8,128)(2,1)} %get-tuple-element.36.refs_3_.refs_4_.refs_6_), custom_call_target="tpu_custom_call" | custom-call | tf_op jit(solution)/shard_map/grid_data/pallas_call | solution.py:357
  23.5 23.7 %exchange.5.refs_0_ = f32[8,2,80,128]{3,2,1,0:T(8,128)} custom-call(f32[8,2,80,128]{3,2,1,0:T(8,128)} %grid_data.1.p_ref), custom_call_target="tpu_custom_call" | custom-call | tf_op jit(solution)/shard_map/exchange/pallas_call | solution.py:228
  47.1 0.4 mul.118
  47.5 2.8 %mul.119 = f32[540,540]{1,0:T(8,128)} reshape(f32[4,135,4,135]{3,2,1,0:T(4,128)S(1)} %mul.118) | data formatting | bytes 2332800 | tf_op jit(solution)/shard_map/mul | solution.py:547
  50.3 2.0 copy.26
  52.3 4.9 %mul.116 = f32[4,4,135,4,135]{4,3,2,1,0:T(4,128)} broadcast(f32[4,4,135,135]{3,2,1,0:T(8,128)S(1)} %copy.26), dimensions={0,1,2,4} | broadcast | bytes 5832000 | tf_op jit(solution)/shard_map/mul | solution.py:547
  57.2 0.0 copy-start
  57.2 9.9 %mul.117 = f32[4,540,540]{2,1,0:T(8,128)} reshape(f32[4,4,135,4,135]{4,3,2,1,0:T(4,128)} %mul.116) | data formatting | bytes 9331200 | tf_op jit(solution)/shard_map/mul | solution.py:547
  67.1 0.0 copy-done
  67.1 6.0 %fusion.1 = (bf16[4,540,540]{2,1,0:T(8,128)(2,1)}, bf16[4,540,540]{2,1,0:T(8,128)(2,1)}) fusion(f32[4,540,540]{2,1,0:T(8,128)} %mul.117, f32[540,540]{1,0:T(8,128)S(1)} %copy-done), kind=kLoop, calls=%fused_computation.5 | loop fusion | flops 5832000 | bytes 10497600 | tf_op jit(solution)/shard_map/convert_element_type | solution.py:144
  73.1 9.2 %fusion = (bf16[4,540,1152]{2,1,0:T(8,128)(2,1)}, bf16[4,540,1152]{2,1,0:T(8,128)(2,1)}) fusion(f32[4,540,1152]{2,0,1:T(4,128)} %param.8), kind=kLoop, calls=%fused_computation.2 | loop fusion | flops 9953280 | bytes 19906560 | tf_op jit(solution)/shard_map/convert_element_type | solution.py:144
  82.4 11.7 %coeff_first.1 = (f32[8,2,80,128]{3,2,1,0:T(8,128)}, f32[4,32,540]{2,1,0:T(8,128)}, f32[4,32,540]{2,1,0:T(8,128)}) custom-call(f32[8,2,80,128]{3,2,1,0:T(8,128)} %exchange.5.refs_0_, bf16[4,540,1152]{2,1,0:T(8,128)(2,1)} %get-tuple-element.31.refs_1_.refs_2_, bf16[4,540,1152]{2,1,0:T(8,128)(2,1)} %get-tuple-element.30.refs_2_.refs_3_, ...), custom_call_target="tpu_custom_call" | custom-call | tf_op jit(solution)/shard_map/coeff_first/pallas_call | solution.py:508
  94.0 22.2 %exchange.6.refs_0_.refs_1_ = f32[8,2,80,128]{3,2,1,0:T(8,128)} custom-call(f32[8,2,80,128]{3,2,1,0:T(8,128)} %get-tuple-element.15.p_ref), custom_call_target="tpu_custom_call" | custom-call | tf_op jit(solution)/shard_map/exchange/pallas_call | solution.py:228
  116.2 14.6 %grid_first.1 = (f32[8,2,80,128]{3,2,1,0:T(8,128)}, f32[8,128]{1,0:T(8,128)}) custom-call(f32[8,2,80,128]{3,2,1,0:T(8,128)} %exchange.6.refs_0_.refs_1_, f32[144,1080]{1,0:T(8,128)} %select_add_fusion.refs_1_.refs_3_, bf16[192,1080]{1,0:T(8,128)(2,1)} %copy.27.refs_2_.refs_4_, bf16[1080,128]{1,0:T(8,128)(2,1)} %get-tuple-element.37.refs_2_.refs_3_.refs_5_, ...), custom_call_target="tpu_custom_call" | custom-call | tf_op jit(solution)/shard_map/grid_first/pallas_call | solution.py:357
  130.9 22.3 %exchange.7.refs_0_ = f32[8,2,80,128]{3,2,1,0:T(8,128)} custom-call(f32[8,2,80,128]{3,2,1,0:T(8,128)} %get-tuple-element.16.p_ref), custom_call_target="tpu_custom_call" | custom-call | tf_op jit(solution)/shard_map/exchange/pallas_call | solution.py:228
  153.2 12.1 %coeff_middle.1 = (f32[8,2,80,128]{3,2,1,0:T(8,128)}, f32[4,32,540]{2,1,0:T(8,128)}, f32[4,32,540]{2,1,0:T(8,128)}, f32[4,32,540]{2,1,0:T(8,128)}) custom-call(f32[8,2,80,128]{3,2,1,0:T(8,128)} %exchange.7.refs_0_, f32[8,128]{1,0:T(8,128)} %get-tuple-element.17.refs_1_.refs_2_, bf16[4,540,1152]{2,1,0:T(8,128)(2,1)} %get-tuple-element.31.refs_1_.refs_2_, ...), custom_call_target="tpu_custom_call" | custom-call | tf_op jit(solution)/shard_map/coeff_middle/pallas_call | solution.py:508
  165.2 22.3 %exchange.8.refs_0_ = f32[8,2,80,128]{3,2,1,0:T(8,128)} custom-call(f32[8,2,80,128]{3,2,1,0:T(8,128)} %get-tuple-element.20.p_ref), custom_call_target="tpu_custom_call" | custom-call | tf_op jit(solution)/shard_map/exchange/pallas_call | solution.py:228
  187.5 14.7 %grid_next.1 = (f32[8,2,80,128]{3,2,1,0:T(8,128)}, f32[8,128]{1,0:T(8,128)}) custom-call(f32[8,2,80,128]{3,2,1,0:T(8,128)} %exchange.8.refs_0_, f32[8,2,80,128]{3,2,1,0:T(8,128)} %exchange.6.refs_0_.refs_1_, f32[8,128]{1,0:T(8,128)} %get-tuple-element.17.refs_1_.refs_2_, f32[144,1080]{1,0:T(8,128)} %select_add_fusion.refs_1_.refs_3_, ...), custom_call_target="tpu_custom_call" | custom-call | tf_op jit(solution)/shard_map/grid_next/pallas_call | solution.py:357
  202.3 22.3 %exchange.9.refs_0_ = f32[8,2,80,128]{3,2,1,0:T(8,128)} custom-call(f32[8,2,80,128]{3,2,1,0:T(8,128)} %get-tuple-element.21.p_ref), custom_call_target="tpu_custom_call" | custom-call | tf_op jit(solution)/shard_map/exchange/pallas_call | solution.py:228
  224.6 8.2 %coeff_last.1 = (f32[4,32,540]{2,1,0:T(8,128)}, f32[4,32,540]{2,1,0:T(8,128)}) custom-call(f32[8,2,80,128]{3,2,1,0:T(8,128)} %exchange.9.refs_0_, f32[8,128]{1,0:T(8,128)} %get-tuple-element.22.refs_1_, bf16[4,540,1152]{2,1,0:T(8,128)(2,1)} %get-tuple-element.31.refs_1_.refs_2_, bf16[4,540,1152]{2,1,0:T(8,128)(2,1)} %get-tuple-element.30.refs_2_.refs_3_, ...), custom_call_target="tpu_custom_call" | custom-call | tf_op jit(solution)/shard_map/coeff_last/pallas_call | solution.py:508
  (6 shorter events, 0.1 us)
Async XLA Ops:
  0.6 7.0 %copy-start.1 = (s32[144,1080]{1,0:T(8,128)S(1)}, s32[144,1080]{1,0:T(8,128)}, u32[]{:S(2)}) copy-start(s32[144,1080]{1,0:T(8,128)} %param.7) | copy-start | bytes 1866244
  57.2 9.9 %copy-start = (f32[540,540]{1,0:T(8,128)S(1)}, f32[540,540]{1,0:T(8,128)}, u32[]{:S(2)}) copy-start(f32[540,540]{1,0:T(8,128)} %mul.119) | copy-start | bytes 3499204

commit v2 on v1

--- a/solution.py
+++ b/solution.py
@@ -14,6 +14,7 @@
 HUBER_LEVELS = (1.0, 0.5, 0.25, 0.125)
 HIGHEST = lax.Precision.HIGHEST
 GROUP = 8
+NEVER = 2**30
 MESH = pl.DeviceIdType.MESH
 VMEM_WHOLE = pl.BlockSpec(memory_space=pltpu.VMEM)
 
@@ -139,11 +140,6 @@
     return high, (values - high.astype(jnp.float32)).astype(jnp.bfloat16)
 
 
-def split_outside(values):
-    high = lax.reduce_precision(values, 8, 7)
-    return high.astype(jnp.bfloat16), (values - high).astype(jnp.bfloat16)
-
-
 def exchange_kernel(
     blocks, p_ref, o_ref, from_core, summed, from_x, ready, send_sem, recv_sem
 ):
@@ -198,11 +194,10 @@
             ready[to] = value
             launch(2, j, ready.at[to], o_ref.at[blk, core, mine], (to, lon))
 
-    for step in range(blocks + 2):
-        if step < blocks:
-            over_x(order[step])
-        if step >= 2:
-            over_blk(order[step - 2])
+    for j in order:
+        over_x(j)
+    for j in order:
+        over_blk(j)
     arrivals = order[-1:] + order[:-1]
     for j in arrivals:
         source = (blk - j + blocks) % blocks
@@ -275,11 +270,11 @@
     return tile
 
 
-def grid_kernel(kind, half, *refs):
-    columns = pl.num_programs(0)
-    n = pl.program_id(0)
+def grid_kernel(kind, half, batch, *refs):
+    steps = pl.num_programs(0)
+    step = pl.program_id(0)
     if kind == "data":
-        field, weights, trig_down, trig_low, p_ref, down = refs
+        field, classes, trig, p_ref, weights, trig_up, trig_down, trig_low, down = refs
     elif kind == "first":
         o_ref, weights, trig_up, trig_down, trig_low, p_ref, q_ref, down, up, cycles = refs
     else:
@@ -287,8 +282,25 @@
          p_ref, q_ref, down, up, cycles) = refs
     blocks, lanes = down.shape[0], down.shape[1]
     group = GROUP
-    if kind != "data":
-        @pl.when(n == 0)
+    cycle_count = 2 * half
+    if kind == "data":
+        @pl.when(step == 0)
+        def _():
+            level = classes[...]
+            weighted = jnp.zeros(level.shape, jnp.float32)
+            for index, value in enumerate(HUBER_LEVELS):
+                weighted = jnp.where(level == index, value, weighted)
+            weights[...] = weighted
+            table = trig[...]
+            high = table.astype(jnp.bfloat16).astype(jnp.float32)
+            rest = table - high
+            trig_up[...] = jnp.concatenate([high, rest, high], axis=0).astype(jnp.bfloat16)
+            trig_down[...] = jnp.concatenate([high, rest], axis=0).T.astype(jnp.bfloat16)
+            trig_low[...] = (
+                jnp.concatenate([high, jnp.zeros_like(high)], axis=0).T.astype(jnp.bfloat16)
+            )
+    else:
+        @pl.when(step == 0)
         def _():
             sums = sums_of(o_ref, half, group)
             if kind == "first":
@@ -310,23 +322,39 @@
                     cycles[b, h * half:(h + 1) * half] = rows
                 up[b] = cycles[b].T
 
-        stack = jnp.concatenate(
-            [up[b, pl.ds(pl.multiple_of(n * group, 8), group), :] for b in range(blocks)], axis=0
-        )
-        high = stack.astype(jnp.bfloat16).astype(jnp.float32)
-        triple = jnp.concatenate([high, high, stack - high], axis=0).T.astype(jnp.bfloat16)
-        grid_field = jnp.dot(triple, trig_up[...], preferred_element_type=jnp.float32)
+    def place(inner):
+        return pl.ds(pl.multiple_of((step * batch + inner) * group, 8), group)
+
+    if kind == "data":
+        grids = [field[inner] for inner in range(batch)]
     else:
-        grid_field = field[0]
-    high, low = split(grid_field * weights[...])
+        triples = []
+        for inner in range(batch):
+            stack = jnp.concatenate(
+                [up[b, place(inner), :] for b in range(blocks)], axis=0
+            )
+            high = stack.astype(jnp.bfloat16).astype(jnp.float32)
+            triple = jnp.concatenate([high, high, stack - high], axis=0)
+            triples.append(triple.T.astype(jnp.bfloat16))
+        fields = jnp.dot(
+            jnp.concatenate(triples, axis=0), trig_up[...], preferred_element_type=jnp.float32
+        )
+        grids = [
+            fields[inner * cycle_count:(inner + 1) * cycle_count] for inner in range(batch)
+        ]
+    scale = weights[...]
+    parts = [split(one * scale) for one in grids]
+    high = jnp.concatenate([part[0] for part in parts], axis=0)
+    low = jnp.concatenate([part[1] for part in parts], axis=0)
     sums = jnp.dot(high, trig_down[...], preferred_element_type=jnp.float32)
     sums = sums + jnp.dot(low, trig_low[...], preferred_element_type=jnp.float32)
-    sums = sums.T
-    sums = sums[: 8 * blocks] + sums[8 * blocks:]
-    for b in range(blocks):
-        down[b, pl.ds(pl.multiple_of(n * group, 8), group), :] = sums[8 * b:8 * b + 8]
-
-    @pl.when(n == columns - 1)
+    for inner in range(batch):
+        turned = sums[inner * cycle_count:(inner + 1) * cycle_count].T
+        turned = turned[: group * blocks] + turned[group * blocks:]
+        for b in range(blocks):
+            down[b, place(inner), :] = turned[group * b:group * (b + 1)]
+
+    @pl.when(step == steps - 1)
     def _():
         total = jnp.zeros((1, lanes), jnp.float32)
         for b in range(blocks):
@@ -345,18 +373,27 @@
 def grid_call(kind, blocks, lanes, cycle_count, rhs_count, *operands):
     half = cycle_count // 2
     padded = -(-(half + 8) // 16) * 16
+    batch = 4 if rhs_count % 4 == 0 else 1
     out_shape = [jax.ShapeDtypeStruct((blocks, 2, padded, lanes), jnp.float32)]
     scratch = [pltpu.VMEM((blocks, lanes, cycle_count), jnp.float32)]
     in_specs = [VMEM_WHOLE] * len(operands)
     if kind == "data":
-        in_specs[0] = pl.BlockSpec((1,) + operands[0].shape[1:], lambda n: (n, 0, 0))
+        shape = operands[0].shape
+        in_specs[0] = pl.BlockSpec((batch,) + shape[1:], lambda n: (n, 0, 0))
+        rows = operands[2].shape[0]
+        out_shape += [
+            jax.ShapeDtypeStruct(shape[1:], jnp.float32),
+            jax.ShapeDtypeStruct((3 * rows, shape[2]), jnp.bfloat16),
+            jax.ShapeDtypeStruct((shape[2], 2 * rows), jnp.bfloat16),
+            jax.ShapeDtypeStruct((shape[2], 2 * rows), jnp.bfloat16),
+        ]
     else:
         out_shape.append(jax.ShapeDtypeStruct((8, lanes), jnp.float32))
         scratch.append(pltpu.VMEM((blocks, lanes, cycle_count), jnp.float32))
         scratch.append(pltpu.VMEM((blocks, cycle_count, lanes), jnp.float32))
     return pl.pallas_call(
-        functools.partial(grid_kernel, kind, half),
-        grid=(rhs_count,),
+        functools.partial(grid_kernel, kind, half, batch),
+        grid=(rhs_count // batch,),
         out_shape=out_shape,
         in_specs=in_specs,
         out_specs=[VMEM_WHOLE] * len(out_shape),
@@ -383,16 +420,31 @@
 NT = (((1,), (1,)), ((), ()))
 
 
+def block_diagonal(blocks_ref):
+    _, count, width, _ = blocks_ref.shape
+    rows = []
+    for index in range(count):
+        parts = []
+        if index:
+            parts.append(jnp.zeros((width, width * index), jnp.float32))
+        parts.append(blocks_ref[0, index])
+        if index + 1 < count:
+            parts.append(jnp.zeros((width, width * (count - 1 - index)), jnp.float32))
+        rows.append(jnp.concatenate(parts, axis=1))
+    return jnp.concatenate(rows, axis=0)
+
+
 def coeff_kernel(kind, half, *refs):
     s = pl.program_id(0)
     if kind == "first":
-        (o_ref, leg_high, leg_low, pre_high, pre_low, live, prior,
-         p_ref, residual, z_out, spread_down, turned_down, tiles, up, dots) = refs
+        (o_ref, places, legendre, precond, prior,
+         p_ref, residual, z_out, leg_high, leg_low, pre_high, pre_low,
+         spread_down, turned_down, tiles, up, dots) = refs
     elif kind == "middle":
-        (o_ref, q_ref, leg_high, leg_low, pre_high, pre_low, live, prior, old, direction,
+        (o_ref, q_ref, leg_high, leg_low, pre_high, pre_low, places, prior, old, direction,
          p_ref, residual, z_out, solution, spread_down, turned_down, tiles, up, dots, alphas) = refs
     else:
-        (o_ref, q_ref, leg_high, leg_low, live, prior, old, direction, z_in, old_solution,
+        (o_ref, q_ref, leg_high, leg_low, places, prior, old, direction, z_in, old_solution,
          residual, solution, spread_down, turned_down, tiles, alphas) = refs
     blocks = o_ref.shape[0]
     lanes = o_ref.shape[3]
@@ -421,9 +473,16 @@
                 alphas[index] = jnp.concatenate([once, once], axis=0)
 
     where = pl.ds(pl.multiple_of(s * rows, rows), rows)
+    if kind == "first":
+        leg_high[0], leg_low[0] = split(legendre[0])
+        pre_high[0], pre_low[0] = split(block_diagonal(precond))
     cycles = turned_down[where, :]
     image = product(cycles, leg_high[0], leg_low[0], NT)
-    mask = live[0]
+    order = places[s]
+    degree = places[pl.num_programs(0)] + lax.broadcasted_iota(jnp.int32, residual.shape[1:], 1)
+    sine = lax.broadcasted_iota(jnp.int32, residual.shape[1:], 0) >= rows // 2
+    least = jnp.where(sine, jnp.maximum(order, jnp.where(order == 0, NEVER, 0)), order)
+    mask = (degree >= least).astype(jnp.float32)
     if kind == "first":
         res = mask * image
     else:
@@ -477,7 +536,7 @@
 
 
 def coeff_call(kind, cycle_count, lanes, *operands):
-    legendre_at = 1 if kind == "first" else 2
+    legendre_at = 2
     slots, degrees, cycles = operands[legendre_at].shape
     rows = lanes // slots
     blocks, _, padded, _ = operands[0].shape
@@ -485,6 +544,10 @@
     for place, operand in enumerate(operands):
         if place >= legendre_at and operand.ndim == 3:
             in_specs.append(pl.BlockSpec((1,) + operand.shape[1:], lambda s: (s, 0, 0)))
+        elif place >= legendre_at and operand.ndim == 4:
+            in_specs.append(pl.BlockSpec((1,) + operand.shape[1:], lambda s: (s, 0, 0, 0)))
+        elif operand.ndim == 1:
+            in_specs.append(pl.BlockSpec(memory_space=pltpu.SMEM))
         else:
             in_specs.append(VMEM_WHOLE)
     vector = jax.ShapeDtypeStruct((slots, rows, degrees), jnp.float32)
@@ -501,6 +564,10 @@
         vectors = 2 if kind == "first" else 3
         out_shape = [partial] + [vector] * vectors
         out_specs = [VMEM_WHOLE] + [vector_spec] * vectors
+        if kind == "first":
+            for shape in ((degrees, cycles), (degrees, degrees)):
+                out_shape += [jax.ShapeDtypeStruct((slots,) + shape, jnp.bfloat16)] * 2
+                out_specs += [pl.BlockSpec((1,) + shape, lambda s: (s, 0, 0))] * 2
         scratch.append(pltpu.VMEM((lanes, cycles), jnp.float32))
         scratch.append(pltpu.VMEM((3, lanes, lanes), jnp.float32))
     if kind != "first":
@@ -530,47 +597,37 @@
     stride_value = local_degrees * lon_count // window
     all_orders = assign * stride_value
     own_orders = lax.dynamic_slice_in_dim(all_orders, blk_place * slot_count, slot_count)
-    live = build_mask(own_orders, lon_place * local_degrees, local_degrees)
-    live = jnp.broadcast_to(live, (slot_count, 2, rhs_count, local_degrees)).reshape(
-        slot_count, 2 * rhs_count, local_degrees
-    )
-    weights = huber_weights(classes)
-    trig = trig_table(
-        all_orders, lon_place * longitudes, longitudes, longitudes * lon_count
-    ).reshape(2 * window, longitudes)
-    trig_high, trig_rest = split_outside(trig)
-    trig_up = jnp.concatenate([trig_high, trig_rest, trig_high], axis=0)
-    trig_down = jnp.concatenate([trig_high, trig_rest], axis=0).T
-    trig_low = jnp.concatenate([trig_high, jnp.zeros_like(trig_high)], axis=0).T
-    leg = split_outside(legendre)
-    per_slot = precond.shape[1]
-    dense = precond[:, :, :, None, :] * jnp.eye(per_slot, dtype=jnp.float32)[None, :, None, :, None]
-    pre = split_outside(dense.reshape(slot_count, local_degrees, local_degrees))
+    places = jnp.concatenate([own_orders, (lon_place * local_degrees)[None]])
+    pair_orders = jnp.repeat(all_orders, 2)[:, None]
+    column = lon_place * longitudes + jnp.arange(longitudes, dtype=jnp.int32)
+    phases = pair_orders * column[None, :] % (longitudes * lon_count)
+    angles = phases.astype(jnp.float32) * (2.0 * math.pi / (longitudes * lon_count))
+    sine = (jnp.arange(2 * window) % 2 == 1)[:, None]
+    trig = jnp.where(sine, jnp.sin(angles), jnp.cos(angles))
     prior_row = prior[None, :]
-    on_grid = functools.partial(grid_call)
 
     sizes = (blocks, lanes, cycle_count, rhs_count)
-    (partial,) = on_grid("data", *sizes, anomalies, weights, trig_down, trig_low)
+    partial, *tables = grid_call("data", *sizes, anomalies, classes, trig)
     sums = exchange(partial)
-    partial, residual, direction = coeff_call(
-        "first", cycle_count, lanes, sums, *leg, *pre, live, prior_row
+    partial, residual, direction, *factors = coeff_call(
+        "first", cycle_count, lanes, sums, places, legendre, precond, prior_row
     )
     first_up = exchange(partial)
-    partial, scalars = on_grid(
-        "first", *sizes, first_up, weights, trig_up, trig_down, trig_low
+    partial, scalars = grid_call(
+        "first", *sizes, first_up, *tables
     )
     sums = exchange(partial)
     partial, residual, search, solved = coeff_call(
-        "middle", cycle_count, lanes, sums, scalars, *leg, *pre, live, prior_row,
+        "middle", cycle_count, lanes, sums, scalars, *factors, places, prior_row,
         residual, direction,
     )
     second_up = exchange(partial)
-    partial, scalars = on_grid(
-        "next", *sizes, second_up, first_up, scalars, weights, trig_up, trig_down, trig_low
+    partial, scalars = grid_call(
+        "next", *sizes, second_up, first_up, scalars, *tables
     )
     sums = exchange(partial)
     residual, solved = coeff_call(
-        "last", cycle_count, lanes, sums, scalars, *leg, live, prior_row,
+        "last", cycle_count, lanes, sums, scalars, *factors[:2], places, prior_row,
         residual, direction, search, solved,
     )
     shape = (slot_count, 2, rhs_count, local_degrees)

time: 234 us -> 178 us (0.76)
  Pallas kernels: 189 us -> 162 us
  other arithmetic: 19.4 us -> 3.35 us
  local copies, waits for them, and re-layouts: 23.9 us -> 11.6 us
    mul x4 -> x1, local copies, waits for them, and re-layouts: 17.9 us -> 0.1 us  [fast_body(): phases = pair_orders * column[None, :] % (longitudes * lon_count)]
    convert_element_type x6 -> x0, other arithmetic: 15.5 us -> none  [the longest x3 15.4 us: split_outside(): return (high.astype(jnp.bfloat16), (values - high).astype(jnp.bfloat16))]
    pallas_call x3, Pallas kernels: 44.1 us -> 28.8 us  [grid_call(): pl.pallas_call(functools.partial(grid_kernel, kind, half, batch), grid=(r...]
    pallas_call x5, Pallas kernels: 113 us -> 98.5 us  [exchange(): pl.pallas_call(functools.partial(exchange_kernel, blocks), out_shape=jax....]
    unnamed x5 -> x4, local copies, waits for them, and re-layouts: 2.03 us -> 10.1 us
    pallas_call x3, Pallas kernels: 31.9 us -> 34.4 us  [coeff_call(): pl.pallas_call(functools.partial(coeff_kernel, kind, cycle_count // 2), g...]
where the time goes in v2:
time: 178 us
  Pallas kernels  162 us (91%)
  local copies, waits for them, and re-layouts  11.6 us (7%)
  other arithmetic  3.35 us (2%)
    pallas_call x5, Pallas kernels, exchange(): pl.pallas_call(functools.partial(exchange_kernel, blocks), out_shape=jax....  98.5 us
    pallas_call x3, Pallas kernels, coeff_call(): pl.pallas_call(functools.partial(coeff_kernel, kind, cycle_count // 2), g...  34.4 us
    pallas_call x3, Pallas kernels, grid_call(): pl.pallas_call(functools.partial(grid_kernel, kind, half, batch), grid=(r...  28.8 us
    unnamed x4, local copies, waits for them, and re-layouts  10.1 us

profile of v2, /device:TPU:0, one launch (start us, length us, event | category | flops | bytes accessed | tf_op | source)
XLA Modules:
  0.0 177.5 jit_solution(2372538243070940952)
XLA Ops:
  0.6 0.7 broadcast_multiply_fusion
  1.3 0.1 dynamic_slice.3
  1.4 0.6 pad_add_fusion.refs_1_.refs_6_.refs_4_
  2.0 1.3 broadcast_in_dim.22.refs_4_.refs_7_.refs_5_
  3.3 0.1 broadcast_in_dim.20
  3.3 0.1 mul.38
  3.4 2.1 %cosine_select_fusion.refs_2_ = f32[64,1080]{1,0:T(8,128)} fusion(s32[1080]{0:T(1024)S(1)} %iota_add_fusion, s32[64]{0:T(128)S(1)} %mul.38, pred[64]{0:T(512)(128)(4,1)S(1)} %fusion.5), kind=kLoop, calls=%fused_computation.3 | loop fusion | flops 691200 | bytes 281120 | tf_op jit(solution)/shard_map/jit(_where)/select_n | solution.py:606
  5.5 0.0 copy-start
  5.5 9.3 %grid_data.1 = (f32[8,2,80,128]{3,2,1,0:T(8,128)}, f32[144,1080]{1,0:T(8,128)}, bf16[192,1080]{1,0:T(8,128)(2,1)}, bf16[1080,128]{1,0:T(8,128)(2,1)}, bf16[1080,128]{1,0:T(8,128)(2,1)}) custom-call(f32[16,144,1080]{2,1,0:T(8,128)} %refs_0_.1, s32[144,1080]{1,0:T(8,128)} %refs_1_.1, f32[64,1080]{1,0:T(8,128)} %cosine_select_fusion.refs_2_), custom_call_target="tpu_custom_call" | custom-call | tf_op jit(solution)/shard_map/grid_data/pallas_call | solution.py:394
  14.8 21.9 %exchange.5.refs_0_ = f32[8,2,80,128]{3,2,1,0:T(8,128)} custom-call(f32[8,2,80,128]{3,2,1,0:T(8,128)} %get-tuple-element.24.p_ref), custom_call_target="tpu_custom_call" | custom-call | tf_op jit(solution)/shard_map/exchange/pallas_call | solution.py:223
  36.7 0.0 copy-done
  36.7 1.8 %copy.11.refs_3_ = f32[4,4,135,135]{3,2,1,0:T(8,128)} copy(f32[4,4,135,135]{3,1,2,0:T(4,128)S(1)} %copy-done) | data formatting | bytes 2332800 | tf_op args[3]
  38.6 8.3 %copy.10.refs_2_ = f32[4,540,1152]{2,1,0:T(8,128)} copy(f32[4,540,1152]{2,0,1:T(4,128)} %param.8) | data formatting | bytes 19906560 | tf_op args[2]
  46.8 14.2 %coeff_first.1 = (f32[8,2,80,128]{3,2,1,0:T(8,128)}, f32[4,32,540]{2,1,0:T(8,128)}, f32[4,32,540]{2,1,0:T(8,128)}, bf16[4,540,1152]{2,1,0:T(8,128)(2,1)}, bf16[4...) custom-call(f32[8,2,80,128]{3,2,1,0:T(8,128)} %exchange.5.refs_0_, ...), custom_call_target="tpu_custom_call" | custom-call | tf_op jit(solution)/shard_map/coeff_first/pallas_call | solution.py:575
  61.1 19.2 %exchange.6.refs_0_.refs_1_ = f32[8,2,80,128]{3,2,1,0:T(8,128)} custom-call(f32[8,2,80,128]{3,2,1,0:T(8,128)} %get-tuple-element.25.p_ref), custom_call_target="tpu_custom_call" | custom-call | tf_op jit(solution)/shard_map/exchange/pallas_call | solution.py:223
  80.3 9.5 %grid_first.1 = (f32[8,2,80,128]{3,2,1,0:T(8,128)}, f32[8,128]{1,0:T(8,128)}) custom-call(f32[8,2,80,128]{3,2,1,0:T(8,128)} %exchange.6.refs_0_.refs_1_, f32[144,1080]{1,0:T(8,128)} %get-tuple-element.26.refs_1_.refs_3_, bf16[192,1080]{1,0:T(8,128)(2,1)} %get-tuple-element.27.refs_2_.refs_4_, bf16[1080,128]{1,0:T(8,128)(2,1)} %get-tuple-element.28.refs_3_.refs_5_, ...), custom_call_target="tpu_custom_call" | custom-call | tf_op jit(solution)/shard_map/grid_first/pallas_call | solution.py:394
  89.8 19.1 %exchange.7.refs_0_ = f32[8,2,80,128]{3,2,1,0:T(8,128)} custom-call(f32[8,2,80,128]{3,2,1,0:T(8,128)} %get-tuple-element.30.p_ref), custom_call_target="tpu_custom_call" | custom-call | tf_op jit(solution)/shard_map/exchange/pallas_call | solution.py:223
  108.9 12.0 %coeff_middle.1 = (f32[8,2,80,128]{3,2,1,0:T(8,128)}, f32[4,32,540]{2,1,0:T(8,128)}, f32[4,32,540]{2,1,0:T(8,128)}, f32[4,32,540]{2,1,0:T(8,128)}) custom-call(f32[8,2,80,128]{3,2,1,0:T(8,128)} %exchange.7.refs_0_, f32[8,128]{1,0:T(8,128)} %get-tuple-element.31.refs_1_.refs_2_, bf16[4,540,1152]{2,1,0:T(8,128)(2,1)} %get-tuple-element.32.refs_2_, ...), custom_call_target="tpu_custom_call" | custom-call | tf_op jit(solution)/shard_map/coeff_middle/pallas_call | solution.py:575
  121.0 19.1 %exchange.8.refs_0_ = f32[8,2,80,128]{3,2,1,0:T(8,128)} custom-call(f32[8,2,80,128]{3,2,1,0:T(8,128)} %get-tuple-element.38.p_ref), custom_call_target="tpu_custom_call" | custom-call | tf_op jit(solution)/shard_map/exchange/pallas_call | solution.py:223
  140.1 9.9 %grid_next.1 = (f32[8,2,80,128]{3,2,1,0:T(8,128)}, f32[8,128]{1,0:T(8,128)}) custom-call(f32[8,2,80,128]{3,2,1,0:T(8,128)} %exchange.8.refs_0_, f32[8,2,80,128]{3,2,1,0:T(8,128)} %exchange.6.refs_0_.refs_1_, f32[8,128]{1,0:T(8,128)} %get-tuple-element.31.refs_1_.refs_2_, f32[144,1080]{1,0:T(8,128)} %get-tuple-element.26.refs_1_.refs_3_, ...), custom_call_target="tpu_custom_call" | custom-call | tf_op jit(solution)/shard_map/grid_next/pallas_call | solution.py:394
  150.0 19.1 %exchange.9.refs_0_ = f32[8,2,80,128]{3,2,1,0:T(8,128)} custom-call(f32[8,2,80,128]{3,2,1,0:T(8,128)} %get-tuple-element.39.p_ref), custom_call_target="tpu_custom_call" | custom-call | tf_op jit(solution)/shard_map/exchange/pallas_call | solution.py:223
  169.2 8.2 %coeff_last.1 = (f32[4,32,540]{2,1,0:T(8,128)}, f32[4,32,540]{2,1,0:T(8,128)}) custom-call(f32[8,2,80,128]{3,2,1,0:T(8,128)} %exchange.9.refs_0_, f32[8,128]{1,0:T(8,128)} %get-tuple-element.40.refs_1_, bf16[4,540,1152]{2,1,0:T(8,128)(2,1)} %get-tuple-element.32.refs_2_, bf16[4,540,1152]{2,1,0:T(8,128)(2,1)} %get-tuple-element.33.refs_3_, ...), custom_call_target="tpu_custom_call" | custom-call | tf_op jit(solution)/shard_map/coeff_last/pallas_call | solution.py:575
  (2 shorter events, 0.0 us)
Async XLA Ops:
  5.5 31.2 %copy-start = (f32[4,4,135,135]{3,1,2,0:T(4,128)S(1)}, f32[4,4,135,135]{3,1,2,0:T(4,128)}, u32[]{:S(2)}) copy-start(f32[4,4,135,135]{3,1,2,0:T(4,128)} %param.9) | copy-start | bytes 3499204

commit v3 on v2

--- a/solution.py
+++ b/solution.py
@@ -140,22 +140,28 @@
     return high, (values - high.astype(jnp.float32)).astype(jnp.bfloat16)
 
 
-def exchange_kernel(
-    blocks, p_ref, o_ref, from_core, summed, from_x, ready, send_sem, recv_sem
-):
+def mates():
     blk = lax.axis_index("blk")
     lon = lax.axis_index("lon")
     core, x = lon % 2, lon // 2
-    core_mate = (blk, lon + 1 - 2 * core)
-    x_mate = (blk, lon + 2 - 4 * x)
-    part = from_x.shape[1]
-    mine = pl.ds(pl.multiple_of(part * x, 8), part)
-    theirs = pl.ds(pl.multiple_of(part * (1 - x), 8), part)
+    return blk, lon, core, x, (blk, lon + 1 - 2 * core), (blk, lon + 2 - 4 * x)
+
+
+def greet(blocks):
+    blk, lon, _, _, core_mate, x_mate = mates()
     barrier = pltpu.get_barrier_semaphore()
     peers = [core_mate, x_mate] + [((blk + j) % blocks, lon) for j in range(1, blocks)]
     for peer in peers:
         pl.semaphore_signal(barrier, inc=1, device_id=peer, device_id_type=MESH)
-    pl.semaphore_wait(barrier, len(peers))
+
+
+def exchange(blocks, p_ref, landed, from_core, summed, from_x, ready, send_sem, recv_sem):
+    blk, lon, core, x, core_mate, x_mate = mates()
+    o_ref = landed
+    pl.semaphore_wait(pltpu.get_barrier_semaphore(), blocks + 1)
+    part = from_x.shape[1]
+    mine = pl.ds(pl.multiple_of(part * x, 8), part)
+    theirs = pl.ds(pl.multiple_of(part * (1 - x), 8), part)
 
     def copy(stage, j, src, dst, peer):
         return pltpu.make_async_remote_copy(
@@ -218,24 +224,17 @@
         one.wait_send()
 
 
-def exchange(partial):
-    blocks, halves, padded, lanes = partial.shape
-    return pl.pallas_call(
-        functools.partial(exchange_kernel, blocks),
-        out_shape=jax.ShapeDtypeStruct(partial.shape, jnp.float32),
-        in_specs=[VMEM_WHOLE],
-        out_specs=VMEM_WHOLE,
-        scratch_shapes=[
-            pltpu.VMEM((blocks, padded, lanes), jnp.float32),
-            pltpu.VMEM((blocks, padded, lanes), jnp.float32),
-            pltpu.VMEM((blocks, padded // 2, lanes), jnp.float32),
-            pltpu.VMEM((blocks, padded // 2, lanes), jnp.float32),
-            pltpu.SemaphoreType.DMA((6, blocks)),
-            pltpu.SemaphoreType.DMA((6, blocks)),
-        ],
-        compiler_params=pltpu.CompilerParams(collective_id=0, has_side_effects=True),
-        name="exchange",
-    )(partial)
+def exchange_scratch(blocks, padded, lanes):
+    return [
+        pltpu.VMEM((blocks, 2, padded, lanes), jnp.float32),
+        pltpu.VMEM((blocks, 2, padded, lanes), jnp.float32),
+        pltpu.VMEM((blocks, padded, lanes), jnp.float32),
+        pltpu.VMEM((blocks, padded, lanes), jnp.float32),
+        pltpu.VMEM((blocks, padded // 2, lanes), jnp.float32),
+        pltpu.VMEM((blocks, padded // 2, lanes), jnp.float32),
+        pltpu.SemaphoreType.DMA((6, blocks)),
+        pltpu.SemaphoreType.DMA((6, blocks)),
+    ]
 
 
 def group_sum(tile, group):
@@ -273,16 +272,22 @@
 def grid_kernel(kind, half, batch, *refs):
     steps = pl.num_programs(0)
     step = pl.program_id(0)
+    refs, p_ref, links = refs[:-8], refs[-8], refs[-7:]
     if kind == "data":
-        field, classes, trig, p_ref, weights, trig_up, trig_down, trig_low, down = refs
+        field, classes, trig, out_ref, weights, trig_up, trig_down, trig_low, down = refs
     elif kind == "first":
-        o_ref, weights, trig_up, trig_down, trig_low, p_ref, q_ref, down, up, cycles = refs
+        o_ref, weights, trig_up, trig_down, trig_low, out_ref, q_ref, down, up, cycles = refs
     else:
         (o_ref, old_ref, old_q, weights, trig_up, trig_down, trig_low,
-         p_ref, q_ref, down, up, cycles) = refs
+         out_ref, q_ref, down, up, cycles) = refs
     blocks, lanes = down.shape[0], down.shape[1]
     group = GROUP
     cycle_count = 2 * half
+
+    @pl.when(step == 0)
+    def _():
+        greet(blocks)
+
     if kind == "data":
         @pl.when(step == 0)
         def _():
@@ -368,6 +373,9 @@
                 p_ref[b, h, half:] = jnp.zeros((p_ref.shape[2] - half, lanes), jnp.float32)
             if kind != "data":
                 p_ref[b, 0, half:half + 8] = tile_of([total])
+        exchange(blocks, p_ref, *links)
+        for b in range(blocks):
+            out_ref[b] = links[0][b]
 
 
 def grid_call(kind, blocks, lanes, cycle_count, rhs_count, *operands):
@@ -391,6 +399,7 @@
         out_shape.append(jax.ShapeDtypeStruct((8, lanes), jnp.float32))
         scratch.append(pltpu.VMEM((blocks, lanes, cycle_count), jnp.float32))
         scratch.append(pltpu.VMEM((blocks, cycle_count, lanes), jnp.float32))
+    scratch += exchange_scratch(blocks, padded, lanes)
     return pl.pallas_call(
         functools.partial(grid_kernel, kind, half, batch),
         grid=(rhs_count // batch,),
@@ -398,7 +407,11 @@
         in_specs=in_specs,
         out_specs=[VMEM_WHOLE] * len(out_shape),
         scratch_shapes=scratch,
-        compiler_params=pltpu.CompilerParams(vmem_limit_bytes=60 << 20),
+        compiler_params=pltpu.CompilerParams(
+            vmem_limit_bytes=60 << 20,
+            collective_id=("data", "first", "next").index(kind),
+            has_side_effects=True,
+        ),
         name="grid_" + kind,
     )(*operands)
 
@@ -436,13 +449,15 @@
 
 def coeff_kernel(kind, half, *refs):
     s = pl.program_id(0)
+    if kind != "last":
+        refs, p_ref, links = refs[:-8], refs[-8], refs[-7:]
     if kind == "first":
         (o_ref, places, legendre, precond, prior,
-         p_ref, residual, z_out, leg_high, leg_low, pre_high, pre_low,
+         out_ref, residual, z_out, leg_high, leg_low, pre_high, pre_low,
          spread_down, turned_down, tiles, up, dots) = refs
     elif kind == "middle":
         (o_ref, q_ref, leg_high, leg_low, pre_high, pre_low, places, prior, old, direction,
-         p_ref, residual, z_out, solution, spread_down, turned_down, tiles, up, dots, alphas) = refs
+         out_ref, residual, z_out, solution, spread_down, turned_down, tiles, up, dots, alphas) = refs
     else:
         (o_ref, q_ref, leg_high, leg_low, places, prior, old, direction, z_in, old_solution,
          residual, solution, spread_down, turned_down, tiles, alphas) = refs
@@ -453,6 +468,8 @@
 
     @pl.when(s == 0)
     def _():
+        if kind != "last":
+            greet(blocks)
         for b in range(blocks):
             for h in range(2):
                 spread_down[(2 * b + h) * half:(2 * b + h + 1) * half, :] = o_ref[b, h, 0:half]
@@ -533,6 +550,9 @@
                 p_ref[b, h, 0:half] = spread_down[at:at + half, :]
                 p_ref[b, h, half:] = jnp.zeros((p_ref.shape[2] - half, lanes), jnp.float32)
             p_ref[b, 0, half:half + 8] = tile
+        exchange(blocks, p_ref, *links)
+        for b in range(blocks):
+            out_ref[b] = links[0][b]
 
 
 def coeff_call(kind, cycle_count, lanes, *operands):
@@ -572,6 +592,10 @@
         scratch.append(pltpu.VMEM((3, lanes, lanes), jnp.float32))
     if kind != "first":
         scratch.append(pltpu.VMEM((2, rows, lanes), jnp.float32))
+    params = {"vmem_limit_bytes": 60 << 20}
+    if kind != "last":
+        scratch += exchange_scratch(blocks, padded, lanes)
+        params.update(collective_id=3 if kind == "first" else 4, has_side_effects=True)
     return pl.pallas_call(
         functools.partial(coeff_kernel, kind, cycle_count // 2),
         grid=(slots,),
@@ -579,7 +603,7 @@
         in_specs=in_specs,
         out_specs=out_specs,
         scratch_shapes=scratch,
-        compiler_params=pltpu.CompilerParams(vmem_limit_bytes=60 << 20),
+        compiler_params=pltpu.CompilerParams(**params),
         name="coeff_" + kind,
     )(*operands)
 
@@ -607,25 +631,16 @@
     prior_row = prior[None, :]
 
     sizes = (blocks, lanes, cycle_count, rhs_count)
-    partial, *tables = grid_call("data", *sizes, anomalies, classes, trig)
-    sums = exchange(partial)
-    partial, residual, direction, *factors = coeff_call(
+    sums, *tables = grid_call("data", *sizes, anomalies, classes, trig)
+    first_up, residual, direction, *factors = coeff_call(
         "first", cycle_count, lanes, sums, places, legendre, precond, prior_row
     )
-    first_up = exchange(partial)
-    partial, scalars = grid_call(
-        "first", *sizes, first_up, *tables
-    )
-    sums = exchange(partial)
-    partial, residual, search, solved = coeff_call(
+    sums, scalars = grid_call("first", *sizes, first_up, *tables)
+    second_up, residual, search, solved = coeff_call(
         "middle", cycle_count, lanes, sums, scalars, *factors, places, prior_row,
         residual, direction,
     )
-    second_up = exchange(partial)
-    partial, scalars = grid_call(
-        "next", *sizes, second_up, first_up, scalars, *tables
-    )
-    sums = exchange(partial)
+    sums, scalars = grid_call("next", *sizes, second_up, first_up, scalars, *tables)
     residual, solved = coeff_call(
         "last", cycle_count, lanes, sums, scalars, *factors[:2], places, prior_row,
         residual, direction, search, solved,

time: 178 us -> 158 us (0.89)
  Pallas kernels: 162 us -> 142 us
    pallas_call x5 -> x0, Pallas kernels: 98.5 us -> none  [exchange(): pl.pallas_call(functools.partial(exchange_kernel, blocks), out_shape=jax....]
    pallas_call x3, Pallas kernels: 28.8 us -> 78.7 us  [grid_call(): pl.pallas_call(functools.partial(grid_kernel, kind, half, batch), grid=(r...]
    pallas_call x3, Pallas kernels: 34.4 us -> 63.1 us  [coeff_call(): pl.pallas_call(functools.partial(coeff_kernel, kind, cycle_count // 2), g...]
where the time goes in v3:
time: 158 us
  Pallas kernels  142 us (90%)
  local copies, waits for them, and re-layouts  11.6 us (7%)
  other arithmetic  3.39 us (2%)
    pallas_call x3, Pallas kernels, grid_call(): pl.pallas_call(functools.partial(grid_kernel, kind, half, batch), grid=(r...  78.7 us
    pallas_call x3, Pallas kernels, coeff_call(): pl.pallas_call(functools.partial(coeff_kernel, kind, cycle_count // 2), g...  63.1 us
    unnamed x4, local copies, waits for them, and re-layouts  10.1 us

profile of v3, /device:TPU:0, one launch (start us, length us, event | category | flops | bytes accessed | tf_op | source)
XLA Modules:
  0.0 157.7 jit_solution(753449519815883859)
XLA Ops:
  0.6 0.7 broadcast_multiply_fusion
  1.3 0.1 dynamic_slice.3
  1.4 0.7 pad_add_fusion.refs_1_.refs_6_.refs_4_
  2.0 1.3 broadcast_in_dim.22.refs_4_.refs_7_.refs_5_
  3.3 0.1 broadcast_in_dim.20
  3.4 0.1 mul.38
  3.5 2.1 %cosine_select_fusion.refs_2_ = f32[64,1080]{1,0:T(8,128)} fusion(s32[1080]{0:T(1024)S(1)} %iota_add_fusion, s32[64]{0:T(128)S(1)} %mul.38, pred[64]{0:T(512)(128)(4,1)S(1)} %fusion.5), kind=kLoop, calls=%fused_computation.3 | loop fusion | flops 691200 | bytes 281120 | tf_op jit(solution)/shard_map/jit(_where)/select_n | solution.py:630
  5.6 0.0 copy-start
  5.6 27.7 %grid_data.1 = (f32[8,2,80,128]{3,2,1,0:T(8,128)}, f32[144,1080]{1,0:T(8,128)}, bf16[192,1080]{1,0:T(8,128)(2,1)}, bf16[1080,128]{1,0:T(8,128)(2,1)}, bf16[1080,128]{1,0:T(8,128)(2,1)}) custom-call(f32[16,144,1080]{2,1,0:T(8,128)} %refs_0_.1, s32[144,1080]{1,0:T(8,128)} %refs_1_.1, f32[64,1080]{1,0:T(8,128)} %cosine_select_fusion.refs_2_), custom_call_target="tpu_custom_call" | custom-call | tf_op jit(solution)/shard_map/grid_data/pallas_call | solution.py:403
  33.2 0.0 copy-done
  33.3 1.8 %copy.11.refs_3_ = f32[4,4,135,135]{3,2,1,0:T(8,128)} copy(f32[4,4,135,135]{3,1,2,0:T(4,128)S(1)} %copy-done) | data formatting | bytes 2332800 | tf_op args[3]
  35.1 8.3 %copy.10.refs_2_ = f32[4,540,1152]{2,1,0:T(8,128)} copy(f32[4,540,1152]{2,0,1:T(4,128)} %param.8) | data formatting | bytes 19906560 | tf_op args[2]
  43.4 28.5 %coeff_first.1 = (f32[8,2,80,128]{3,2,1,0:T(8,128)}, f32[4,32,540]{2,1,0:T(8,128)}, f32[4,32,540]{2,1,0:T(8,128)}, bf16[4,540,1152]{2,1,0:T(8,128)(2,1)}, bf16[4...) custom-call(f32[8,2,80,128]{3,2,1,0:T(8,128)} %get-tuple-element.24.refs_0_, ...), custom_call_target="tpu_custom_call" | custom-call | tf_op jit(solution)/shard_map/coeff_first/pallas_call | solution.py:599
  71.9 25.3 %grid_first.1 = (f32[8,2,80,128]{3,2,1,0:T(8,128)}, f32[8,128]{1,0:T(8,128)}) custom-call(f32[8,2,80,128]{3,2,1,0:T(8,128)} %get-tuple-element.25.refs_0_.refs_1_, f32[144,1080]{1,0:T(8,128)} %get-tuple-element.26.refs_1_.refs_3_, bf16[192,1080]{1,0:T(8,128)(2,1)} %get-tuple-element.27.refs_2_.refs_4_, bf16[1080,128]{1,0:T(8,128)(2,1)} %get-tuple-element.28.refs_3_.refs_5_, ...), custom_call_target="tpu_custom_call" | custom-call | tf_op jit(solution)/shard_map/grid_first/pallas_call | solution.py:403
  97.2 26.4 %coeff_middle.1 = (f32[8,2,80,128]{3,2,1,0:T(8,128)}, f32[4,32,540]{2,1,0:T(8,128)}, f32[4,32,540]{2,1,0:T(8,128)}, f32[4,32,540]{2,1,0:T(8,128)}) custom-call(f32[8,2,80,128]{3,2,1,0:T(8,128)} %get-tuple-element.30.refs_0_, f32[8,128]{1,0:T(8,128)} %get-tuple-element.31.refs_1_.refs_2_, bf16[4,540,1152]{2,1,0:T(8,128)(2,1)} %get-tuple-element.32.refs_2_, ...), custom_call_target="tpu_custom_call" | custom-call | tf_op jit(solution)/shard_map/coeff_middle/pallas_call | solution.py:599
  123.6 25.7 %grid_next.1 = (f32[8,2,80,128]{3,2,1,0:T(8,128)}, f32[8,128]{1,0:T(8,128)}) custom-call(f32[8,2,80,128]{3,2,1,0:T(8,128)} %get-tuple-element.38.refs_0_, f32[8,2,80,128]{3,2,1,0:T(8,128)} %get-tuple-element.25.refs_0_.refs_1_, f32[8,128]{1,0:T(8,128)} %get-tuple-element.31.refs_1_.refs_2_, f32[144,1080]{1,0:T(8,128)} %get-tuple-element.26.refs_1_.refs_3_, ...), custom_call_target="tpu_custom_call" | custom-call | tf_op jit(solution)/shard_map/grid_next/pallas_call | solution.py:403
  149.4 8.2 %coeff_last.1 = (f32[4,32,540]{2,1,0:T(8,128)}, f32[4,32,540]{2,1,0:T(8,128)}) custom-call(f32[8,2,80,128]{3,2,1,0:T(8,128)} %get-tuple-element.39.refs_0_, f32[8,128]{1,0:T(8,128)} %get-tuple-element.40.refs_1_, bf16[4,540,1152]{2,1,0:T(8,128)(2,1)} %get-tuple-element.32.refs_2_, bf16[4,540,1152]{2,1,0:T(8,128)(2,1)} %get-tuple-element.33.refs_3_, ...), custom_call_target="tpu_custom_call" | custom-call | tf_op jit(solution)/shard_map/coeff_last/pallas_call | solution.py:599
  (2 shorter events, 0.0 us)
Async XLA Ops:
  5.6 27.7 %copy-start = (f32[4,4,135,135]{3,1,2,0:T(4,128)S(1)}, f32[4,4,135,135]{3,1,2,0:T(4,128)}, u32[]{:S(2)}) copy-start(f32[4,4,135,135]{3,1,2,0:T(4,128)} %param.9) | copy-start | bytes 3499204

commit v4 on v3

--- a/solution.py
+++ b/solution.py
@@ -155,7 +155,8 @@
         pl.semaphore_signal(barrier, inc=1, device_id=peer, device_id_type=MESH)
 
 
-def exchange(blocks, p_ref, landed, from_core, summed, from_x, ready, send_sem, recv_sem):
+def exchange(blocks, p_ref, landed, from_core, summed, from_x, ready, send_sem, recv_sem,
+             between=lambda: None):
     blk, lon, core, x, core_mate, x_mate = mates()
     o_ref = landed
     pl.semaphore_wait(pltpu.get_barrier_semaphore(), blocks + 1)
@@ -204,6 +205,7 @@
         over_x(j)
     for j in order:
         over_blk(j)
+    between()
     arrivals = order[-1:] + order[:-1]
     for j in arrivals:
         source = (blk - j + blocks) % blocks
@@ -274,7 +276,8 @@
     step = pl.program_id(0)
     refs, p_ref, links = refs[:-8], refs[-8], refs[-7:]
     if kind == "data":
-        field, classes, trig, out_ref, weights, trig_up, trig_down, trig_low, down = refs
+        (field, classes, trig, turned_leg, out_ref, weights, trig_up, trig_down, trig_low, leg_out,
+         down, leg_buffer, leg_sem) = refs
     elif kind == "first":
         o_ref, weights, trig_up, trig_down, trig_low, out_ref, q_ref, down, up, cycles = refs
     else:
@@ -289,8 +292,22 @@
         greet(blocks)
 
     if kind == "data":
+        def fetch(slot):
+            return pltpu.make_async_copy(
+                turned_leg.at[:, slot, :], leg_buffer.at[slot], leg_sem.at[0, slot]
+            )
+
+        def store(slot):
+            return pltpu.make_async_copy(
+                leg_buffer.at[slot], leg_out.at[slot], leg_sem.at[1, slot]
+            )
+
+        slots = range(leg_buffer.shape[0])
+
         @pl.when(step == 0)
         def _():
+            for slot in slots:
+                fetch(slot).start()
             level = classes[...]
             weighted = jnp.zeros(level.shape, jnp.float32)
             for index, value in enumerate(HUBER_LEVELS):
@@ -373,9 +390,18 @@
                 p_ref[b, h, half:] = jnp.zeros((p_ref.shape[2] - half, lanes), jnp.float32)
             if kind != "data":
                 p_ref[b, 0, half:half + 8] = tile_of([total])
-        exchange(blocks, p_ref, *links)
+        def relay():
+            if kind == "data":
+                for slot in slots:
+                    fetch(slot).wait()
+                    store(slot).start()
+
+        exchange(blocks, p_ref, *links, between=relay)
         for b in range(blocks):
             out_ref[b] = links[0][b]
+        if kind == "data":
+            for slot in slots:
+                store(slot).wait()
 
 
 def grid_call(kind, blocks, lanes, cycle_count, rhs_count, *operands):
@@ -389,23 +415,31 @@
         shape = operands[0].shape
         in_specs[0] = pl.BlockSpec((batch,) + shape[1:], lambda n: (n, 0, 0))
         rows = operands[2].shape[0]
+        degrees, slots, cycles = operands[3].shape
+        in_specs[3] = pl.BlockSpec(memory_space=pl.ANY)
         out_shape += [
             jax.ShapeDtypeStruct(shape[1:], jnp.float32),
             jax.ShapeDtypeStruct((3 * rows, shape[2]), jnp.bfloat16),
             jax.ShapeDtypeStruct((shape[2], 2 * rows), jnp.bfloat16),
             jax.ShapeDtypeStruct((shape[2], 2 * rows), jnp.bfloat16),
+            jax.ShapeDtypeStruct((slots, degrees, cycles), jnp.float32),
         ]
+        scratch.append(pltpu.VMEM((slots, degrees, cycles), jnp.float32))
+        scratch.append(pltpu.SemaphoreType.DMA((2, slots)))
     else:
         out_shape.append(jax.ShapeDtypeStruct((8, lanes), jnp.float32))
         scratch.append(pltpu.VMEM((blocks, lanes, cycle_count), jnp.float32))
         scratch.append(pltpu.VMEM((blocks, cycle_count, lanes), jnp.float32))
     scratch += exchange_scratch(blocks, padded, lanes)
+    out_specs = [VMEM_WHOLE] * len(out_shape)
+    if kind == "data":
+        out_specs[-1] = pl.BlockSpec(memory_space=pl.ANY)
     return pl.pallas_call(
         functools.partial(grid_kernel, kind, half, batch),
         grid=(rhs_count // batch,),
         out_shape=out_shape,
         in_specs=in_specs,
-        out_specs=[VMEM_WHOLE] * len(out_shape),
+        out_specs=out_specs,
         scratch_shapes=scratch,
         compiler_params=pltpu.CompilerParams(
             vmem_limit_bytes=60 << 20,
@@ -631,9 +665,11 @@
     prior_row = prior[None, :]
 
     sizes = (blocks, lanes, cycle_count, rhs_count)
-    sums, *tables = grid_call("data", *sizes, anomalies, classes, trig)
+    sums, *tables, ordered = grid_call(
+        "data", *sizes, anomalies, classes, trig, legendre.transpose(1, 0, 2)
+    )
     first_up, residual, direction, *factors = coeff_call(
-        "first", cycle_count, lanes, sums, places, legendre, precond, prior_row
+        "first", cycle_count, lanes, sums, places, ordered, precond, prior_row
     )
     sums, scalars = grid_call("first", *sizes, first_up, *tables)
     second_up, residual, search, solved = coeff_call(

time: 158 us -> 153 us (0.968)
  local copies, waits for them, and re-layouts: 11.6 us -> 4.98 us
    unnamed x4 -> x1, local copies, waits for them, and re-layouts: 10.1 us -> 3.45 us
where the time goes in v4:
time: 153 us; the launch traced here: 152 us
  Pallas kernels  143 us (93%)
  local copies, waits for them, and re-layouts  4.98 us (3%)
  other arithmetic  3.35 us (2%)
    pallas_call x3, Pallas kernels, grid_call(): pl.pallas_call(functools.partial(grid_kernel, kind, half, batch), grid=(r...  80.1 us
    pallas_call x3, Pallas kernels, coeff_call(): pl.pallas_call(functools.partial(coeff_kernel, kind, cycle_count // 2), g...  63.2 us
    unnamed x1, local copies, waits for them, and re-layouts  3.45 us

profile of v4, /device:TPU:0, one launch (start us, length us, event | category | flops | bytes accessed | tf_op | source)
XLA Modules:
  0.0 152.4 jit_solution(18431513840065748245)
XLA Ops:
  0.6 0.7 broadcast_multiply_fusion
  1.3 0.1 dynamic_slice.3
  1.4 0.6 pad_add_fusion.refs_1_.refs_6_.refs_4_
  2.0 1.3 broadcast_in_dim.22.refs_4_.refs_7_.refs_5_
  3.3 0.1 broadcast_in_dim.20
  3.4 0.1 mul.38
  3.5 2.1 %cosine_select_fusion.refs_2_ = f32[64,1080]{1,0:T(8,128)} fusion(s32[1080]{0:T(1024)S(1)} %iota_add_fusion, s32[64]{0:T(128)S(1)} %mul.38, pred[64]{0:T(512)(128)(4,1)S(1)} %fusion.5), kind=kLoop, calls=%fused_computation.3 | loop fusion | flops 691200 | bytes 281120 | tf_op jit(solution)/shard_map/jit(_where)/select_n | solution.py:664
  5.5 3.4 %copy.9.refs_3_ = f32[4,4,135,135]{3,2,1,0:T(8,128)} copy(f32[4,4,135,135]{3,1,2,0:T(4,128)} %param.9) | data formatting | bytes 2332800 | tf_op args[3]
  9.0 29.1 %grid_data.1 = (f32[8,2,80,128]{3,2,1,0:T(8,128)}, f32[144,1080]{1,0:T(8,128)}, bf16[192,1080]{1,0:T(8,128)(2,1)}, bf16[1080,128]{1,0:T(8,128)(2,1)}, bf16[1080,...) custom-call(f32[16,144,1080]{2,1,0:T(8,128)} %refs_0_.1, s32[144,1080]{1,0:T(8,128)} %refs_1_.1, ...), custom_call_target="tpu_custom_call" | custom-call | tf_op jit(solution)/shard_map/grid_data/pallas_call | solution.py:437
  38.0 28.6 %coeff_first.1 = (f32[8,2,80,128]{3,2,1,0:T(8,128)}, f32[4,32,540]{2,1,0:T(8,128)}, f32[4,32,540]{2,1,0:T(8,128)}, bf16[4,540,1152]{2,1,0:T(8,128)(2,1)}, bf16[4...) custom-call(f32[8,2,80,128]{3,2,1,0:T(8,128)} %get-tuple-element.25.refs_0_, ...), custom_call_target="tpu_custom_call" | custom-call | tf_op jit(solution)/shard_map/coeff_first/pallas_call | solution.py:633
  66.6 25.3 %grid_first.1 = (f32[8,2,80,128]{3,2,1,0:T(8,128)}, f32[8,128]{1,0:T(8,128)}) custom-call(f32[8,2,80,128]{3,2,1,0:T(8,128)} %get-tuple-element.27.refs_0_.refs_1_, f32[144,1080]{1,0:T(8,128)} %get-tuple-element.28.refs_1_.refs_3_, bf16[192,1080]{1,0:T(8,128)(2,1)} %get-tuple-element.29.refs_2_.refs_4_, bf16[1080,128]{1,0:T(8,128)(2,1)} %get-tuple-element.30.refs_3_.refs_5_, ...), custom_call_target="tpu_custom_call" | custom-call | tf_op jit(solution)/shard_map/grid_first/pallas_call | solution.py:437
  91.9 26.4 %coeff_middle.1 = (f32[8,2,80,128]{3,2,1,0:T(8,128)}, f32[4,32,540]{2,1,0:T(8,128)}, f32[4,32,540]{2,1,0:T(8,128)}, f32[4,32,540]{2,1,0:T(8,128)}) custom-call(f32[8,2,80,128]{3,2,1,0:T(8,128)} %get-tuple-element.32.refs_0_, f32[8,128]{1,0:T(8,128)} %get-tuple-element.33.refs_1_.refs_2_, bf16[4,540,1152]{2,1,0:T(8,128)(2,1)} %get-tuple-element.34.refs_2_, ...), custom_call_target="tpu_custom_call" | custom-call | tf_op jit(solution)/shard_map/coeff_middle/pallas_call | solution.py:633
  118.3 25.7 %grid_next.1 = (f32[8,2,80,128]{3,2,1,0:T(8,128)}, f32[8,128]{1,0:T(8,128)}) custom-call(f32[8,2,80,128]{3,2,1,0:T(8,128)} %get-tuple-element.40.refs_0_, f32[8,2,80,128]{3,2,1,0:T(8,128)} %get-tuple-element.27.refs_0_.refs_1_, f32[8,128]{1,0:T(8,128)} %get-tuple-element.33.refs_1_.refs_2_, f32[144,1080]{1,0:T(8,128)} %get-tuple-element.28.refs_1_.refs_3_, ...), custom_call_target="tpu_custom_call" | custom-call | tf_op jit(solution)/shard_map/grid_next/pallas_call | solution.py:437
  144.1 8.2 %coeff_last.1 = (f32[4,32,540]{2,1,0:T(8,128)}, f32[4,32,540]{2,1,0:T(8,128)}) custom-call(f32[8,2,80,128]{3,2,1,0:T(8,128)} %get-tuple-element.41.refs_0_, f32[8,128]{1,0:T(8,128)} %get-tuple-element.42.refs_1_, bf16[4,540,1152]{2,1,0:T(8,128)(2,1)} %get-tuple-element.34.refs_2_, bf16[4,540,1152]{2,1,0:T(8,128)(2,1)} %get-tuple-element.35.refs_3_, ...), custom_call_target="tpu_custom_call" | custom-call | tf_op jit(solution)/shard_map/coeff_last/pallas_call | solution.py:633
  (2 shorter events, 0.0 us)
